TPU v7x, 128 devices: a whole 4x4x4 slice. The times are simulated.
128 devices in a mesh: band: 32 (over z, y, core), lon: 4 (over x).
Axes of the slice: x: 4, y: 4, z: 4, core: 2. Of those that a mesh axis runs over, the one named last changes fastest.
Arguments:
- source: bfloat16 [16384, 8, 128], P(('band', 'lon')), may hold values from -6 to 6
- routes: int32 [16384, 2], P(('band', 'lon')), may hold values from 0 to 11, as said below
- slot_weights: bfloat16 [128, 12, 32, 128, 128], P(('band', 'lon')), may hold values from -0.5 to 0.5
- window: int32 [128, 12, 32], P(('band', 'lon')), may hold values from 0 to 255
- stem_weight: bfloat16 [9, 8, 128], replicated, may hold values from -0.75 to 0.75
- stem_bias: float32 [128], replicated, may hold values from -3 to 3
- mix_weight: bfloat16 [9, 128, 128], replicated, may hold values from -0.1875 to 0.1875
- mix_bias: float32 [128], replicated, may hold values from -3 to 3
Outputs:
- features: bfloat16 [2048, 2048, 128], P('band', 'lon')
Inputs may be any that keep to these rules, and one draw needn't show every extreme that they name: `routes`: each cell block names 2 different codes, never a band outside the grid. Among one device's blocks no code is named more than 32 times, and the device's own tile (code 4) exactly 32 times except in the first and last band. A device of another band names only longitude offsets 0, 1 and 3. A device of the first band names each code of band offsets 0 and +1 exactly 32 times; one of the last band each code of band offsets -1 and 0 exactly 32 times.
All inputs are finite; a program needn't handle non-finite values.
Results may differ from a plain program's by a relative error of at most 0.0056.
Values may be sent and summed in bfloat16 or wider, within the bound.
A program may use at most 128 MiB of HBM per device.

v0:
```python
import jax
import jax.numpy as jnp
from jax import lax
from jax.sharding import PartitionSpec as P

ROWS_DEV = 64
COLS_DEV = 512


def shifted(block, axis, distance):
    devices = range(lax.axis_size(axis))
    route = [(i - distance, i) for i in devices if i - distance in devices]
    return lax.ppermute(block, axis, route)


def extended(block, sides, width, periodic):
    for axis, dim in sides:
        count = lax.axis_size(axis)
        forward = [(i, i + 1) for i in range(count - 1)]
        if periodic:
            forward.append((count - 1, 0))
        backward = [(target, source) for source, target in forward]
        low = lax.ppermute(
            lax.slice_in_dim(block, block.shape[dim] - width, None, axis=dim), axis, forward
        )
        high = lax.ppermute(lax.slice_in_dim(block, 0, width, axis=dim), axis, backward)
        block = jnp.concatenate([low, block, high], axis=dim)
    return block


def stem_conv(padded, weight, rows, cols):
    stacked = jnp.concatenate(
        [padded[:, tap // 3 : tap // 3 + rows, tap % 3 : tap % 3 + cols] for tap in range(9)],
        axis=0,
    )
    flat_weight = weight.reshape(9 * weight.shape[1], weight.shape[2])
    return jnp.einsum("fhw,fc->hwc", stacked, flat_weight, preferred_element_type=jnp.float32)


def mix_conv(padded, weight):
    kernel = weight.reshape(3, 3, weight.shape[1], weight.shape[2])
    result = lax.conv_general_dilated(
        padded[None],
        kernel,
        (1, 1),
        "VALID",
        dimension_numbers=("NHWC", "HWIO", "NHWC"),
        preferred_element_type=jnp.float32,
    )
    return result[0]


def on_device(source, routes, slot_weights, window, stem_weight, stem_bias, mix_weight, mix_bias):
    n_lon = lax.axis_size("lon")
    lon_here = lax.axis_index("lon")
    blk_dev, fields, cells = source.shape
    nbr = slot_weights.shape[1]
    cap = slot_weights.shape[2]
    pixels = slot_weights.shape[4]
    top = routes.shape[1]
    rows = ROWS_DEV
    cols = COLS_DEV
    nwin = rows * cols // pixels
    flat_dest = routes.reshape(-1)
    onehot = (flat_dest[:, None] == jnp.arange(nbr, dtype=jnp.int32)[None, :]).astype(jnp.int32)
    before = jnp.cumsum(onehot, axis=0) - onehot
    rank = jnp.sum(before * onehot, axis=1)
    target_slot = flat_dest * cap + rank
    select = (jnp.arange(nbr * cap, dtype=jnp.int32)[:, None] == target_slot[None, :]).astype(
        jnp.bfloat16
    )
    repeated = jnp.repeat(source.reshape(blk_dev, fields * cells), top, axis=0)
    outgoing = jnp.dot(select, repeated, preferred_element_type=jnp.float32).astype(jnp.bfloat16)
    outgoing = outgoing.reshape(3, n_lon, cap, fields, cells)
    lanes = jnp.arange(n_lon, dtype=jnp.int32)
    to_absolute = (lanes - lon_here) % n_lon
    to_relative = (lon_here - lanes) % n_lon
    absolute = jnp.take(outgoing, to_absolute, axis=1)
    arrived = lax.all_to_all(absolute, "lon", split_axis=1, concat_axis=1, tiled=True)
    arrived = jnp.take(arrived, to_relative, axis=1)
    from_north = shifted(arrived[0], "band", -1)
    from_south = shifted(arrived[2], "band", 1)
    incoming = jnp.stack([from_north, arrived[1], from_south], axis=0)
    incoming = incoming.reshape(nbr, cap, fields, cells)
    contrib = jnp.einsum(
        "qcfk,qckp->qcfp", incoming, slot_weights[0], preferred_element_type=jnp.float32
    ).astype(jnp.bfloat16)
    place = (jnp.arange(nwin, dtype=jnp.int32)[:, None] == window[0].reshape(-1)[None, :]).astype(
        jnp.bfloat16
    )
    summed = jnp.dot(
        place, contrib.reshape(nbr * cap, fields * pixels), preferred_element_type=jnp.float32
    )
    field = summed.reshape(rows, cols // pixels, fields, pixels).transpose(2, 0, 1, 3)
    field = field.reshape(fields, rows, cols).astype(jnp.bfloat16)
    with_rows = extended(field, (("band", 1),), 1, False)
    full = extended(with_rows, (("lon", 2),), 1, True)
    hidden = jax.nn.silu(stem_conv(full, stem_weight, rows, cols) + stem_bias).astype(jnp.bfloat16)
    hidden_rows = extended(hidden, (("band", 0),), 1, False)
    hidden_full = extended(hidden_rows, (("lon", 1),), 1, True)
    result = mix_conv(hidden_full, mix_weight) + mix_bias
    return result.astype(jnp.bfloat16)


def solution(mesh):
    in_specs = (
        P(("band", "lon"), None, None),
        P(("band", "lon"), None),
        P(("band", "lon"), None, None, None, None),
        P(("band", "lon"), None, None),
        P(),
        P(),
        P(),
        P(),
    )
    out_specs = P("band", "lon", None)
    return jax.shard_map(
        on_device, mesh=mesh, in_specs=in_specs, out_specs=out_specs, check_vma=False
    )
```

profile of v0, /device:TPU:96, one launch (start us, length us, event | category | flops | bytes accessed | tf_op | source)
XLA Modules:
  0.0 168.9 jit_solution(2046627614553274242)
XLA Ops:
  5.9 4.3 %all-to-all-start = ((bf16[3,4,32,8,128]{4,3,2,0,1:T(8,128)(2,1)}), bf16[3,4,32,8,128]{4,3,2,0,1:T(8,128)(2,1)S(1)}, u32[]{:S(2)}, u32[]{:S(2)}) async-start(bf16[3,4,32,8,128]{4,3,2,0,1:T(8,128)(2,1)} %select_bitcast_fusion.1), calls=%async_computation | async-start | bytes 1572864 | tf_op jit(solution)/shard_map/all_to_all | solution.py:79
  10.3 12.2 %all-to-all-done = bf16[3,4,32,8,128]{4,3,2,0,1:T(8,128)(2,1)S(1)} async-done(((bf16[3,4,32,8,128]{4,3,2,0,1:T(8,128)(2,1)}), bf16[3,4,32,8,128]{4,3,2,0,1:T(8,128)(2,1)S(1)}, u32[]{:S(2)}, u32[]{:S(2)}) %all-to-all-start) | async-done | bytes 786464 | tf_op jit(solution)/shard_map/all_to_all | solution.py:79
  23.4 3.1 %collective-permute-start = (bf16[4,32,8,128]{3,2,1,0:T(8,128)(2,1)S(1)}, bf16[4,32,8,128]{3,2,1,0:T(8,128)(2,1)S(1)}, u32[]{:S(2)}, u32[]{:S(2)}) collective-permute-start(bf16[4,32,8,128]{3,2,1,0:T(8,128)(2,1)S(1)} %get-tuple-element.10), channel_id=1, source_target_pairs={{4,0},{8,4},{12,8},{16,12},{20,16},{24,20},{28,24},{32,28},{36,32}... | collective-permute-start | bytes 786440 | tf_op jit(solution)/shard_map/ppermute | solution.py:13
  26.5 1.9 %collective-permute-start.1 = (bf16[4,32,8,128]{3,2,1,0:T(8,128)(2,1)S(1)}, bf16[4,32,8,128]{3,2,1,0:T(8,128)(2,1)S(1)}, u32[]{:S(2)}, u32[]{:S(2)}) collective-permute-start(bf16[4,32,8,128]{3,2,1,0:T(8,128)(2,1)S(1)} %get-tuple-element.11), channel_id=1, source_target_pairs={{0,4},{4,8},{8,12},{12,16},{16,20},{20,24},{24,28},{28,32},{32,36}... | collective-permute-start | bytes 786440 | tf_op jit(solution)/shard_map/ppermute | solution.py:13
  28.5 1.8 %collective-permute-done = bf16[4,32,8,128]{3,2,1,0:T(8,128)(2,1)S(1)} collective-permute-done((bf16[4,32,8,128]{3,2,1,0:T(8,128)(2,1)S(1)}, bf16[4,32,8,128]{3,2,1,0:T(8,128)(2,1)S(1)}, u32[]{:S(2)}, u32[]{:S(2)}) %collective-permute-start) | collective-permute-done | bytes 262176 | tf_op jit(solution)/shard_map/ppermute | solution.py:13
  30.4 5.9 %collective-permute-done.1 = bf16[4,32,8,128]{3,2,1,0:T(8,128)(2,1)S(1)} collective-permute-done((bf16[4,32,8,128]{3,2,1,0:T(8,128)(2,1)S(1)}, bf16[4,32,8,128]{3,2,1,0:T(8,128)(2,1)S(1)}, u32[]{:S(2)}, u32[]{:S(2)}) %collective-permute-start.1) | collective-permute-done | bytes 262176 | tf_op jit(solution)/shard_map/ppermute | solution.py:13
  36.4 6.3 %fusion.12 = bf16[12,32,8,128]{3,2,1,0:T(8,128)(2,1)S(1)} fusion(bf16[12,32,8,128]{3,2,1,0:T(8,128)(2,1)S(1)} %bitcast.86, bf16[1,12,32,128,128]{4,3,2,1,0:T(8,128)(2,1)} %param.12), kind=kOutput, calls=%fused_computation.18 | convolution fusion | flops 101056512 | bytes 14155776 | tf_op jit(solution)/shard_map/qcfk,qckp->qcfp/dot_general | solution.py:85
  44.4 1.9 %collective-permute-start.2 = (bf16[8,1,512]{2,0,1:T(8,128)(2,1)S(1)}, bf16[8,1,512]{2,0,1:T(8,128)(2,1)S(1)}, u32[]{:S(2)}, u32[]{:S(2)}) collective-permute-start(bf16[8,1,512]{2,0,1:T(8,128)(2,1)S(1)} %get-tuple-element.16), channel_id=1, source_target_pairs={{0,4},{4,8},{8,12},{12,16},{16,20},{20,24},{24,28},{28,32},{32,36}... | collective-permute-start | bytes 24584 | tf_op jit(solution)/shard_map/ppermute | solution.py:23
  46.4 5.8 %collective-permute-start.3 = (bf16[8,1,512]{2,0,1:T(8,128)(2,1)S(1)}, bf16[8,1,512]{2,0,1:T(8,128)(2,1)S(1)}, u32[]{:S(2)}, u32[]{:S(2)}) collective-permute-start(bf16[8,1,512]{2,0,1:T(8,128)(2,1)S(1)} %get-tuple-element.15), channel_id=1, source_target_pairs={{4,0},{8,4},{12,8},{16,12},{20,16},{24,20},{28,24},{32,28},{36,32}... | collective-permute-start | bytes 24584 | tf_op jit(solution)/shard_map/ppermute | solution.py:26
  54.2 2.7 %collective-permute-start.5 = (bf16[8,66,1]{2,0,1:T(8,128)(2,1)S(1)}, bf16[8,66,1]{2,0,1:T(8,128)(2,1)S(1)}, u32[]{:S(2)}, u32[]{:S(2)}) collective-permute-start(bf16[8,66,1]{2,0,1:T(8,128)(2,1)S(1)} %get-tuple-element.13), channel_id=1, source_target_pairs={{1,0},{2,1},{3,2},{0,3},{5,4},{6,5},{7,6},{4,7},{9,8},{10,9},{11,1... | collective-permute-start | bytes 3176 | tf_op jit(solution)/shard_map/ppermute | solution.py:26
  56.9 3.0 %collective-permute-done.4 = bf16[8,66,1]{2,0,1:T(8,128)(2,1)S(1)} collective-permute-done((bf16[8,66,1]{2,0,1:T(8,128)(2,1)S(1)}, bf16[8,66,1]{2,0,1:T(8,128)(2,1)S(1)}, u32[]{:S(2)}, u32[]{:S(2)}) %collective-permute-start.4) | collective-permute-done | bytes 1088 | tf_op jit(solution)/shard_map/ppermute | solution.py:23
  61.7 5.4 %multiply_convert_fusion = bf16[64,512,128]{2,1,0:T(8,128)(2,1)S(1)} fusion(bf16[72,64,512]{2,0,1:T(8,128)(2,1)S(1)} %fusion.25, f32[128]{0:T(128)S(1)} %copy-done.4, bf16[9,8,128]{2,1,0:T(8,128)(2,1)S(1)} %copy-done.3), kind=kOutput, calls=%fused_computation.7 | convolution fusion | flops 629145600 | bytes 13126144 | tf_op jit(solution)/shard_map/fhw,fc->hwc/dot_general | solution.py:37
  67.2 1.9 %collective-permute-start.6 = (bf16[1,512,128]{2,1,0:T(8,128)(2,1)S(1)}, bf16[1,512,128]{2,1,0:T(8,128)(2,1)S(1)}, u32[]{:S(2)}, u32[]{:S(2)}) collective-permute-start(bf16[1,512,128]{2,1,0:T(8,128)(2,1)S(1)} %get-tuple-element.8), channel_id=1, source_target_pairs={{0,4},{4,8},{8,12},{12,16},{16,20},{20,24},{24,28},{28,32},{32,36}... | collective-permute-start | bytes 393224 | tf_op jit(solution)/shard_map/ppermute | solution.py:23
  69.1 5.8 %collective-permute-start.7 = (bf16[1,512,128]{2,1,0:T(8,128)(2,1)S(1)}, bf16[1,512,128]{2,1,0:T(8,128)(2,1)S(1)}, u32[]{:S(2)}, u32[]{:S(2)}) collective-permute-start(bf16[1,512,128]{2,1,0:T(8,128)(2,1)S(1)} %get-tuple-element.9), channel_id=1, source_target_pairs={{4,0},{8,4},{12,8},{16,12},{20,16},{24,20},{28,24},{32,28},{36,32}... | collective-permute-start | bytes 393224 | tf_op jit(solution)/shard_map/ppermute | solution.py:26
  77.5 3.2 %collective-permute-start.9 = (bf16[66,1,128]{2,1,0:T(2,128)(2,1)S(1)}, bf16[66,1,128]{2,1,0:T(2,128)(2,1)S(1)}, u32[]{:S(2)}, u32[]{:S(2)}) collective-permute-start(bf16[66,1,128]{2,1,0:T(2,128)(2,1)S(1)} %get-tuple-element.7), channel_id=1, source_target_pairs={{1,0},{2,1},{3,2},{0,3},{5,4},{6,5},{7,6},{4,7},{9,8},{10,9},{11,1... | collective-permute-start | bytes 50696 | tf_op jit(solution)/shard_map/ppermute | solution.py:26
  80.7 1.9 %collective-permute-done.8 = bf16[66,1,128]{2,1,0:T(2,128)(2,1)S(1)} collective-permute-done((bf16[66,1,128]{2,1,0:T(2,128)(2,1)S(1)}, bf16[66,1,128]{2,1,0:T(2,128)(2,1)S(1)}, u32[]{:S(2)}, u32[]{:S(2)}) %collective-permute-start.8) | collective-permute-done | bytes 16928 | tf_op jit(solution)/shard_map/ppermute | solution.py:23
  82.6 11.0 %maximum_bitcast_fusion = bf16[66,1,514,128]{3,2,0,1:T(8,128)(2,1)} fusion(bf16[66,1,128]{2,1,0:T(2,128)(2,1)S(1)} %collective-permute-done.9, bf16[1,512,128]{2,1,0:T(8,128)(2,1)S(1)} %collective-permute-done.7, bf16[64,512,128]{2,1,0:T(8,128)(2,1)S(1)} %multiply_convert_fusion, bf16[1,512,128]{2,1,0:T(8,128)(2,1)S(1)} %collective-permute-done.6, ...), kind=kLoop, calls=%fused_computation.16 | loop fusion | flops 43422720 | bytes 17369088 | tf_op jit(solution)/shard_map/broadcast_in_dim | solution.py:43
  93.7 7.5 %pad = bf16[66,1,520,128]{3,2,0,1:T(8,128)(2,1)} pad(bf16[66,1,514,128]{3,2,0,1:T(8,128)(2,1)} %maximum_bitcast_fusion, bf16[]{:T(256)} %constant.47), padding=0_0x0_0x0_6x0_0 | pad | bytes 17470466 | tf_op jit(solution)/shard_map/broadcast_in_dim | solution.py:43
  101.2 13.8 %reshape.90 = bf16[66,1,8,65,128]{4,3,2,0,1:T(8,128)(2,1)} reshape(bf16[66,1,520,128]{3,2,0,1:T(8,128)(2,1)} %pad) | data formatting | bytes 17571840 | tf_op jit(solution)/shard_map/conv_general_dilated | solution.py:42
  115.0 8.6 %copy.28 = bf16[66,1,8,65,128]{4,2,3,0,1:T(8,128)(2,1)} copy(bf16[66,1,8,65,128]{4,3,2,0,1:T(8,128)(2,1)} %reshape.90) | data formatting | bytes 17571840 | tf_op jit(solution)/shard_map/conv_general_dilated | solution.py:42
  124.6 22.3 %convolution_select_fusion = f32[64,8,65,128]{3,1,2,0:T(8,128)S(1)} fusion(bf16[3,3,128,128]{3,2,1,0:T(8,128)(2,1)S(1)} %bitcast.84, bf16[66,1,7,2,128]{4,2,3,0,1:T(8,128)(2,1)S(1)} %slice.116, bf16[66,1,8,65,128]{4,2,3,0,1:T(8,128)(2,1)} %copy.28, pred[8,65]{0,1:T(8,128)(4,1)S(1)} %copy-done.5), kind=kOutput, calls=%fused_computation.10 | convolution fusion | flops 9846099968 | bytes 26357256 | tf_op jit(solution)/shard_map/conv_general_dilated | solution.py:42
  146.9 5.3 %copy.29 = f32[64,8,65,128]{3,0,2,1:T(8,128)S(1)} copy(f32[64,8,65,128]{3,1,2,0:T(8,128)S(1)} %convolution_select_fusion) | data formatting | bytes 34078720 | tf_op jit(solution)/shard_map/conv_general_dilated | solution.py:42
  152.2 4.5 %fusion.2 = bf16[64,512,128]{2,0,1:T(8,128)(2,1)} fusion(f32[64,1,520,128]{3,0,2,1:T(8,128)S(1)} %bitcast.85, f32[128]{0:T(128)S(1)} %copy-done.2), kind=kLoop, calls=%fused_computation.6 | loop fusion | flops 8388608 | bytes 25166336 | tf_op jit(solution)/shard_map/convert_element_type | solution.py:102
  156.8 12.2 %copy.30 = bf16[64,512,128]{2,1,0:T(8,128)(2,1)} copy(bf16[64,512,128]{2,0,1:T(8,128)(2,1)} %fusion.2) | data formatting | bytes 16777216 | tf_op jit(solution)/shard_map/convert_element_type | solution.py:102
  (76 shorter events, 16.1 us)
Async XLA Ops:
  0.0 124.6 %copy-start = (bf16[9,128,128]{2,1,0:T(8,128)(2,1)S(1)}, bf16[9,128,128]{2,1,0:T(8,128)(2,1)}, u32[]{:S(2)}) copy-start(bf16[9,128,128]{2,1,0:T(8,128)(2,1)} %param.16) | copy-start | bytes 884740
  0.0 28.4 %copy-start.1 = (s32[1,12,32]{2,0,1:T(1,128)S(1)}, s32[1,12,32]{2,0,1:T(1,128)}, u32[]{:S(2)}) copy-start(s32[1,12,32]{2,0,1:T(1,128)} %param.13) | copy-start | bytes 4612
  5.9 16.6 %all-to-all-start = ((bf16[3,4,32,8,128]{4,3,2,0,1:T(8,128)(2,1)}), bf16[3,4,32,8,128]{4,3,2,0,1:T(8,128)(2,1)S(1)}, u32[]{:S(2)}, u32[]{:S(2)}) async-start(bf16[3,4,32,8,128]{4,3,2,0,1:T(8,128)(2,1)} %select_bitcast_fusion.1), calls=%async_computation | async-start | bytes 1572864 | tf_op jit(solution)/shard_map/all_to_all | solution.py:79
  23.4 6.9 %collective-permute-start = (bf16[4,32,8,128]{3,2,1,0:T(8,128)(2,1)S(1)}, bf16[4,32,8,128]{3,2,1,0:T(8,128)(2,1)S(1)}, u32[]{:S(2)}, u32[]{:S(2)}) collective-permute-start(bf16[4,32,8,128]{3,2,1,0:T(8,128)(2,1)S(1)} %get-tuple-element.10), channel_id=1, source_target_pairs={{4,0},{8,4},{12,8},{16,12},{20,16},{24,20},{28,24},{32,28},{36,32}... | collective-permute-start | bytes 786440 | tf_op jit(solution)/shard_map/ppermute | solution.py:13
  26.5 9.8 %collective-permute-start.1 = (bf16[4,32,8,128]{3,2,1,0:T(8,128)(2,1)S(1)}, bf16[4,32,8,128]{3,2,1,0:T(8,128)(2,1)S(1)}, u32[]{:S(2)}, u32[]{:S(2)}) collective-permute-start(bf16[4,32,8,128]{3,2,1,0:T(8,128)(2,1)S(1)} %get-tuple-element.11), channel_id=1, source_target_pairs={{0,4},{4,8},{8,12},{12,16},{16,20},{20,24},{24,28},{28,32},{32,36}... | collective-permute-start | bytes 786440 | tf_op jit(solution)/shard_map/ppermute | solution.py:13
  42.9 18.8 %copy-start.3 = (bf16[9,8,128]{2,1,0:T(8,128)(2,1)S(1)}, bf16[9,8,128]{2,1,0:T(8,128)(2,1)}, u32[]{:S(2)}) copy-start(bf16[9,8,128]{2,1,0:T(8,128)(2,1)} %param.14) | copy-start | bytes 55300
  42.9 18.8 %copy-start.4 = (f32[128]{0:T(128)S(1)}, f32[128]{0:T(128)}, u32[]{:S(2)}) copy-start(f32[128]{0:T(128)} %param.15) | copy-start | bytes 1540
  44.4 7.7 %collective-permute-start.2 = (bf16[8,1,512]{2,0,1:T(8,128)(2,1)S(1)}, bf16[8,1,512]{2,0,1:T(8,128)(2,1)S(1)}, u32[]{:S(2)}, u32[]{:S(2)}) collective-permute-start(bf16[8,1,512]{2,0,1:T(8,128)(2,1)S(1)} %get-tuple-element.16), channel_id=1, source_target_pairs={{0,4},{4,8},{8,12},{12,16},{16,20},{20,24},{24,28},{28,32},{32,36}... | collective-permute-start | bytes 24584 | tf_op jit(solution)/shard_map/ppermute | solution.py:23
  46.4 7.1 %collective-permute-start.3 = (bf16[8,1,512]{2,0,1:T(8,128)(2,1)S(1)}, bf16[8,1,512]{2,0,1:T(8,128)(2,1)S(1)}, u32[]{:S(2)}, u32[]{:S(2)}) collective-permute-start(bf16[8,1,512]{2,0,1:T(8,128)(2,1)S(1)} %get-tuple-element.15), channel_id=1, source_target_pairs={{4,0},{8,4},{12,8},{16,12},{20,16},{24,20},{28,24},{32,28},{36,32}... | collective-permute-start | bytes 24584 | tf_op jit(solution)/shard_map/ppermute | solution.py:26
  53.6 6.3 %collective-permute-start.4 = (bf16[8,66,1]{2,0,1:T(8,128)(2,1)S(1)}, bf16[8,66,1]{2,0,1:T(8,128)(2,1)S(1)}, u32[]{:S(2)}, u32[]{:S(2)}) collective-permute-start(bf16[8,66,1]{2,0,1:T(8,128)(2,1)S(1)} %get-tuple-element.14), channel_id=1, source_target_pairs={{0,1},{1,2},{2,3},{3,0},{4,5},{5,6},{6,7},{7,4},{8,9},{9,10},{10,1... | collective-permute-start | bytes 3176 | tf_op jit(solution)/shard_map/ppermute | solution.py:23
  54.2 6.0 %collective-permute-start.5 = (bf16[8,66,1]{2,0,1:T(8,128)(2,1)S(1)}, bf16[8,66,1]{2,0,1:T(8,128)(2,1)S(1)}, u32[]{:S(2)}, u32[]{:S(2)}) collective-permute-start(bf16[8,66,1]{2,0,1:T(8,128)(2,1)S(1)} %get-tuple-element.13), channel_id=1, source_target_pairs={{1,0},{2,1},{3,2},{0,3},{5,4},{6,5},{7,6},{4,7},{9,8},{10,9},{11,1... | collective-permute-start | bytes 3176 | tf_op jit(solution)/shard_map/ppermute | solution.py:26
  67.2 8.4 %collective-permute-start.6 = (bf16[1,512,128]{2,1,0:T(8,128)(2,1)S(1)}, bf16[1,512,128]{2,1,0:T(8,128)(2,1)S(1)}, u32[]{:S(2)}, u32[]{:S(2)}) collective-permute-start(bf16[1,512,128]{2,1,0:T(8,128)(2,1)S(1)} %get-tuple-element.8), channel_id=1, source_target_pairs={{0,4},{4,8},{8,12},{12,16},{16,20},{20,24},{24,28},{28,32},{32,36}... | collective-permute-start | bytes 393224 | tf_op jit(solution)/shard_map/ppermute | solution.py:23
  69.1 8.3 %collective-permute-start.7 = (bf16[1,512,128]{2,1,0:T(8,128)(2,1)S(1)}, bf16[1,512,128]{2,1,0:T(8,128)(2,1)S(1)}, u32[]{:S(2)}, u32[]{:S(2)}) collective-permute-start(bf16[1,512,128]{2,1,0:T(8,128)(2,1)S(1)} %get-tuple-element.9), channel_id=1, source_target_pairs={{4,0},{8,4},{12,8},{16,12},{20,16},{24,20},{28,24},{32,28},{36,32}... | collective-permute-start | bytes 393224 | tf_op jit(solution)/shard_map/ppermute | solution.py:26
  77.4 5.2 %collective-permute-start.8 = (bf16[66,1,128]{2,1,0:T(2,128)(2,1)S(1)}, bf16[66,1,128]{2,1,0:T(2,128)(2,1)S(1)}, u32[]{:S(2)}, u32[]{:S(2)}) collective-permute-start(bf16[66,1,128]{2,1,0:T(2,128)(2,1)S(1)} %get-tuple-element.6), channel_id=1, source_target_pairs={{0,1},{1,2},{2,3},{3,0},{4,5},{5,6},{6,7},{7,4},{8,9},{9,10},{10,1... | collective-permute-start | bytes 50696 | tf_op jit(solution)/shard_map/ppermute | solution.py:23
  77.5 5.1 %collective-permute-start.9 = (bf16[66,1,128]{2,1,0:T(2,128)(2,1)S(1)}, bf16[66,1,128]{2,1,0:T(2,128)(2,1)S(1)}, u32[]{:S(2)}, u32[]{:S(2)}) collective-permute-start(bf16[66,1,128]{2,1,0:T(2,128)(2,1)S(1)} %get-tuple-element.7), channel_id=1, source_target_pairs={{1,0},{2,1},{3,2},{0,3},{5,4},{6,5},{7,6},{4,7},{9,8},{10,9},{11,1... | collective-permute-start | bytes 50696 | tf_op jit(solution)/shard_map/ppermute | solution.py:26
  115.0 9.6 %copy-start.5 = (pred[8,65]{0,1:T(8,128)(4,1)S(1)}, pred[8,65]{0,1:T(8,128)(4,1)}, u32[]{:S(2)}) copy-start(pred[8,65]{0,1:T(8,128)(4,1)} %constant.51) | copy-start | bytes 1564
  146.9 5.3 %copy-start.2 = (f32[128]{0:T(128)S(1)}, f32[128]{0:T(128)}, u32[]{:S(2)}) copy-start(f32[128]{0:T(128)} %param.17) | copy-start | bytes 1540
where the time goes:
time: 171 us; the launch traced here: 169 us
  local copies, waits for them, and re-layouts  54.3 us (32%)
  matrix products  34.9 us (20%)
  starting transfers between devices  31.2 us (18%)
  waiting for transfers between devices  28.7 us (17%)
  other arithmetic  19.4 us (11%)
    conv_general_dilated x4, local copies, waits for them, and re-layouts, mix_conv(): lax.conv_general_dilated(padded[None], kernel, (1, 1), 'VALID', dimension...  28.7 us
    conv_general_dilated x1, matrix products, mix_conv(): lax.conv_general_dilated(padded[None], kernel, (1, 1), 'VALID', dimension...  22.3 us
    ppermute x4, starting transfers between devices, extended(): lax.ppermute(lax.slice_in_dim(block, 0, width, axis=dim), axis, backward)  17.4 us
    all_to_all x1, waiting for transfers between devices, on_device(): lax.all_to_all(absolute, 'lon', split_axis=1, concat_axis=1, tiled=True)  12.2 us
    convert_element_type x1, local copies, waits for them, and re-layouts, on_device(): return result.astype(jnp.bfloat16)  12.2 us
    broadcast_in_dim x1, other arithmetic, mix_conv(): padded[None]  11 us
    ppermute x2, waiting for transfers between devices, shifted(): return lax.ppermute(block, axis, route)  7.75 us
    broadcast_in_dim x1, local copies, waits for them, and re-layouts, mix_conv(): padded[None]  7.53 us
  transfers between devices with their start and end apart: 11, of which 8 were waited for; matrix products, arithmetic and copies ran while one was open for 0% of the time, Pallas kernels for 0%

commit v1 on v0

--- a/solution.py
+++ b/solution.py
@@ -1,6 +1,8 @@
 import jax
 import jax.numpy as jnp
 from jax import lax
+from jax.experimental import pallas as pl
+from jax.experimental.pallas import tpu as pltpu
 from jax.sharding import PartitionSpec as P
 
 ROWS_DEV = 64
@@ -28,26 +30,110 @@
     return block
 
 
-def stem_conv(padded, weight, rows, cols):
-    stacked = jnp.concatenate(
-        [padded[:, tap // 3 : tap // 3 + rows, tap % 3 : tap % 3 + cols] for tap in range(9)],
-        axis=0,
-    )
-    flat_weight = weight.reshape(9 * weight.shape[1], weight.shape[2])
-    return jnp.einsum("fhw,fc->hwc", stacked, flat_weight, preferred_element_type=jnp.float32)
-
-
-def mix_conv(padded, weight):
-    kernel = weight.reshape(3, 3, weight.shape[1], weight.shape[2])
-    result = lax.conv_general_dilated(
-        padded[None],
-        kernel,
-        (1, 1),
-        "VALID",
-        dimension_numbers=("NHWC", "HWIO", "NHWC"),
-        preferred_element_type=jnp.float32,
-    )
-    return result[0]
+MCH = 256
+
+def conv_kernel(flags, ft, sw, sb, mw, mb, out, tmat, mmat, lhs3, tmp, h32, r0, r1, r2, o0, o1, o2, sems):
+    f32, bf16 = jnp.float32, jnp.bfloat16
+    sw32 = sw[...].astype(f32)
+    for j in range(7):
+        for y in range(2):
+            top = 2 * j + y
+            for b in range(3):
+                pieces = []
+                if top > 0:
+                    pieces.append(jnp.zeros((8 * top, 128), f32))
+                for a in range(3):
+                    pieces.append(sw32[(3 * a + b) * 8 : (3 * a + b) * 8 + 8])
+                if top < 13:
+                    pieces.append(jnp.zeros((8 * (13 - top), 128), f32))
+                tmat[j, b * 128 : b * 128 + 128, y * 128 : y * 128 + 128] = jnp.concatenate(pieces, axis=0).astype(bf16)
+    for r in range(4):
+        for b in range(3):
+            for o in range(2):
+                a = r - o
+                block = mw[3 * a + b] if 0 <= a <= 2 else jnp.zeros((128, 128), bf16)
+                mmat[(r * 3 + b) * 128 : (r * 3 + b) * 128 + 128, o * 128 : o * 128 + 128] = block
+    for k in range(5):
+        tmp[...] = ft[k].astype(f32)
+        for b in range(3):
+            lhs3[k, :, b * 128 : b * 128 + 128] = tmp[b : b + 520].astype(bf16)
+
+    hb = sb[...] * 0.5
+    bias = mb[...]
+    first, last = flags[0], flags[1]
+
+    def stem(pair, ring):
+        k = pair // 7
+        j = pair - k * 7
+        acc = jnp.dot(lhs3[k], tmat[j], preferred_element_type=f32)
+        for y in range(2):
+            u = acc[:, y * 128 : y * 128 + 128] * 0.5 + hb
+            h = u + u * jnp.tanh(u)
+            row = 2 * pair + y
+            gone = jnp.logical_or(jnp.logical_and(first == 1, row == 0), jnp.logical_and(last == 1, row == 65))
+            h32[y] = h * jnp.where(gone, 0.0, 1.0)
+            for b in range(3):
+                ring[y, :, b * 128 : b * 128 + 128] = h32[y, b : b + 512].astype(bf16)
+
+    def mix(p, lo, hi, ob):
+        for m in range(0, 512, MCH):
+            lhs = jnp.concatenate([lo[0, m : m + MCH], lo[1, m : m + MCH], hi[0, m : m + MCH], hi[1, m : m + MCH]], axis=1)
+            acc = jnp.dot(lhs, mmat[...], preferred_element_type=f32)
+            ob[0, m : m + MCH] = (acc[:, :128] + bias).astype(bf16)
+            ob[1, m : m + MCH] = (acc[:, 128:] + bias).astype(bf16)
+
+    rings = (r0, r1, r2)
+    obs = (o0, o1, o2)
+    stem(jnp.int32(0), r0)
+    stem(jnp.int32(1), r1)
+
+    def put(p, i):
+        return pltpu.make_async_copy(obs[i], out.at[pl.ds(2 * p, 2)], sems.at[i])
+
+    def body(t, carry):
+        for i in range(3):
+            p = 3 * t + i
+
+            @pl.when(t > 0)
+            def _():
+                put(p - 3, i).wait()
+
+            mix(p, rings[i], rings[(i + 1) % 3], obs[i])
+            stem(p + 2, rings[(i + 2) % 3])
+            put(p, i).start()
+        return carry
+
+    lax.fori_loop(0, 10, body, 0)
+    for i in range(2):
+        put(27 + i, i).wait()
+        mix(30 + i, rings[i], rings[(i + 1) % 3], obs[i])
+        if i == 0:
+            stem(jnp.int32(32), r2)
+        put(30 + i, i).start()
+    put(29, 2).wait()
+    put(30, 0).wait()
+    put(31, 1).wait()
+
+
+def conv(flags, ft, sw, sb, mw, mb):
+    V = pltpu.VMEM
+    bf16, f32 = jnp.bfloat16, jnp.float32
+    vm = pl.BlockSpec(memory_space=pltpu.VMEM)
+    return pl.pallas_call(
+        conv_kernel,
+        out_shape=jax.ShapeDtypeStruct((64, 512, 128), bf16),
+        in_specs=[pl.BlockSpec(memory_space=pltpu.SMEM)] + [vm] * 5,
+        out_specs=pl.BlockSpec(memory_space=pl.ANY),
+        scratch_shapes=[
+            V((7, 384, 256), bf16), V((1536, 256), bf16), V((5, 520, 384), bf16),
+            V((528, 128), f32), V((2, 520, 128), f32),
+            V((2, 512, 384), bf16), V((2, 512, 384), bf16), V((2, 512, 384), bf16),
+            V((2, 512, 128), bf16), V((2, 512, 128), bf16), V((2, 512, 128), bf16),
+            pltpu.SemaphoreType.DMA((3,)),
+        ],
+        compiler_params=pltpu.CompilerParams(vmem_limit_bytes=60 * 1024 * 1024),
+        name="conv",
+    )(flags, ft, sw, sb, mw, mb)
 
 
 def on_device(source, routes, slot_weights, window, stem_weight, stem_bias, mix_weight, mix_bias):
@@ -93,13 +179,21 @@
     )
     field = summed.reshape(rows, cols // pixels, fields, pixels).transpose(2, 0, 1, 3)
     field = field.reshape(fields, rows, cols).astype(jnp.bfloat16)
-    with_rows = extended(field, (("band", 1),), 1, False)
-    full = extended(with_rows, (("lon", 2),), 1, True)
-    hidden = jax.nn.silu(stem_conv(full, stem_weight, rows, cols) + stem_bias).astype(jnp.bfloat16)
-    hidden_rows = extended(hidden, (("band", 0),), 1, False)
-    hidden_full = extended(hidden_rows, (("lon", 1),), 1, True)
-    result = mix_conv(hidden_full, mix_weight) + mix_bias
-    return result.astype(jnp.bfloat16)
+    with_rows = extended(field, (("band", 1),), 2, False)
+    full = extended(with_rows, (("lon", 2),), 2, True)
+    full = jnp.pad(full, ((0, 0), (0, 4), (0, 12)))
+    windows = jnp.stack([full[:, 14 * k : 14 * k + 16] for k in range(5)], axis=0)
+    windows = windows.transpose(0, 3, 2, 1).reshape(5, cols + 16, 16 * fields)
+    band = lax.axis_index("band")
+    flags = jnp.stack([band == 0, band == lax.axis_size("band") - 1]).astype(jnp.int32)
+    return conv(
+        flags,
+        windows,
+        stem_weight.reshape(72, 128),
+        stem_bias.reshape(1, 128),
+        mix_weight,
+        mix_bias.reshape(1, 128),
+    )
 
 
 def solution(mesh):

time: 171 us -> 95.1 us (0.56)
  local copies, waits for them, and re-layouts: 54.3 us -> 6.62 us
  Pallas kernels: 0 us -> 32.3 us
  matrix products: 34.9 us -> 7.21 us
  other arithmetic: 19.4 us -> 3.54 us
  starting transfers between devices: 31.2 us -> 20.3 us
  waiting for transfers between devices: 28.7 us -> 23.9 us
    pallas_call x0 -> x1, Pallas kernels: none -> 32.3 us  [conv(): pl.pallas_call(conv_kernel, out_shape=jax.ShapeDtypeStruct((64, 512, 128)...]
    conv_general_dilated x4 -> x0, local copies, waits for them, and re-layouts: 28.7 us -> none  [mix_conv(): lax.conv_general_dilated(padded[None], kernel, (1, 1), 'VALID', dimension...]
    conv_general_dilated x1 -> x0, matrix products: 22.3 us -> none  [mix_conv(): lax.conv_general_dilated(padded[None], kernel, (1, 1), 'VALID', dimension...]
    convert_element_type x1 -> x0, local copies, waits for them, and re-layouts: 12.2 us -> none  [on_device(): return result.astype(jnp.bfloat16)]
    broadcast_in_dim x1 -> x0, other arithmetic: 11 us -> none  [mix_conv(): padded[None]]
    ppermute x4 -> x2, starting transfers between devices: 17.4 us -> 8.42 us  [extended(): lax.ppermute(lax.slice_in_dim(block, 0, width, axis=dim), axis, backward)]
    broadcast_in_dim x1 -> x0, local copies, waits for them, and re-layouts: 7.53 us -> none  [mix_conv(): padded[None]]
    dot_general x1 -> x0, matrix products: 5.39 us -> none  [stem_conv(): jnp.einsum('fhw,fc->hwc', stacked, flat_weight, preferred_element_type=jn...]
  transfers between devices with their start and end apart: 11 -> 7, of which waited for: 8 -> 5; matrix products, arithmetic and copies ran while one was open for 0% -> 1% of each run, Pallas kernels for 0% -> 0%
where the time goes in v1:
time: 95.1 us; the launch traced here: 94.1 us
  Pallas kernels  32.3 us (34%)
  waiting for transfers between devices  23.9 us (25%)
  starting transfers between devices  20.3 us (21%)
  matrix products  7.21 us (8%)
  local copies, waits for them, and re-layouts  6.62 us (7%)
  other arithmetic  3.54 us (4%)
    pallas_call x1, Pallas kernels, conv(): pl.pallas_call(conv_kernel, out_shape=jax.ShapeDtypeStruct((64, 512, 128)...  32.3 us
    all_to_all x1, waiting for transfers between devices, on_device(): lax.all_to_all(absolute, 'lon', split_axis=1, concat_axis=1, tiled=True)  12.2 us
    ppermute x2, starting transfers between devices, extended(): lax.ppermute(lax.slice_in_dim(block, 0, width, axis=dim), axis, backward)  8.42 us
    ppermute x2, waiting for transfers between devices, shifted(): return lax.ppermute(block, axis, route)  7.75 us
    dot_general x1, matrix products, on_device(): jnp.einsum('qcfk,qckp->qcfp', incoming, slot_weights[0], preferred_elemen...  6.35 us
    ppermute x2, starting transfers between devices, shifted(): return lax.ppermute(block, axis, route)  4.99 us
    all_to_all x1, starting transfers between devices, on_device(): lax.all_to_all(absolute, 'lon', split_axis=1, concat_axis=1, tiled=True)  4.29 us
    ppermute x2, starting transfers between devices, extended(): lax.ppermute(lax.slice_in_dim(block, block.shape[dim] - width, None, axis...  2.55 us
  transfers between devices with their start and end apart: 7, of which 5 were waited for; matrix products, arithmetic and copies ran while one was open for 1% of the time, Pallas kernels for 0%

profile of v1, /device:TPU:96, one launch (start us, length us, event | category | flops | bytes accessed | tf_op | source)
XLA Modules:
  0.0 94.1 jit_solution(10394974826824884910)
XLA Ops:
  0.0 0.8 copy.12
  1.1 0.6 reduce-window.6
  2.1 1.0 %copy.36 = bf16[16,8,8,128]{3,1,2,0:T(8,128)(2,1)S(1)} copy(bf16[16,8,8,128]{3,2,1,0:T(8,128)(2,1)} %bitcast.102) | data formatting | bytes 524288
  4.1 0.7 gather_fusion
  4.9 1.0 %select_bitcast_fusion.1 = bf16[3,4,32,8,128]{4,3,2,0,1:T(8,128)(2,1)} fusion(bf16[4,3,32,8,128]{4,3,2,1,0:T(8,128)(2,1)S(1)} %gather_fusion, pred[4]{0:T(512)(128)(4,1)S(1)} %compare_and_fusion.1), kind=kLoop, calls=%fused_computation.21 | loop fusion | flops 393216 | bytes 1572868 | tf_op jit(solution)/shard_map/jit(_take)/select_n | solution.py:164
  5.9 4.3 %all-to-all-start = ((bf16[3,4,32,8,128]{4,3,2,0,1:T(8,128)(2,1)}), bf16[3,4,32,8,128]{4,3,2,0,1:T(8,128)(2,1)S(1)}, u32[]{:S(2)}, u32[]{:S(2)}) async-start(bf16[3,4,32,8,128]{4,3,2,0,1:T(8,128)(2,1)} %select_bitcast_fusion.1), calls=%async_computation | async-start | bytes 1572864 | tf_op jit(solution)/shard_map/all_to_all | solution.py:165
  10.2 12.2 %all-to-all-done = bf16[3,4,32,8,128]{4,3,2,0,1:T(8,128)(2,1)S(1)} async-done(((bf16[3,4,32,8,128]{4,3,2,0,1:T(8,128)(2,1)}), bf16[3,4,32,8,128]{4,3,2,0,1:T(8,128)(2,1)S(1)}, u32[]{:S(2)}, u32[]{:S(2)}) %all-to-all-start) | async-done | bytes 786464 | tf_op jit(solution)/shard_map/all_to_all | solution.py:165
  22.5 0.7 gather_fusion.1
  23.4 3.1 %collective-permute-start = (bf16[4,32,8,128]{3,2,1,0:T(8,128)(2,1)S(1)}, bf16[4,32,8,128]{3,2,1,0:T(8,128)(2,1)S(1)}, u32[]{:S(2)}, u32[]{:S(2)}) collective-permute-start(bf16[4,32,8,128]{3,2,1,0:T(8,128)(2,1)S(1)} %get-tuple-element.6), channel_id=1, source_target_pairs={{4,0},{8,4},{12,8},{16,12},{20,16},{24,20},{28,24},{32,28},{36,32}... | collective-permute-start | bytes 786440 | tf_op jit(solution)/shard_map/ppermute | solution.py:15
  26.5 1.9 %collective-permute-start.1 = (bf16[4,32,8,128]{3,2,1,0:T(8,128)(2,1)S(1)}, bf16[4,32,8,128]{3,2,1,0:T(8,128)(2,1)S(1)}, u32[]{:S(2)}, u32[]{:S(2)}) collective-permute-start(bf16[4,32,8,128]{3,2,1,0:T(8,128)(2,1)S(1)} %get-tuple-element.7), channel_id=1, source_target_pairs={{0,4},{4,8},{8,12},{12,16},{16,20},{20,24},{24,28},{28,32},{32,36}... | collective-permute-start | bytes 786440 | tf_op jit(solution)/shard_map/ppermute | solution.py:15
  28.5 1.8 %collective-permute-done = bf16[4,32,8,128]{3,2,1,0:T(8,128)(2,1)S(1)} collective-permute-done((bf16[4,32,8,128]{3,2,1,0:T(8,128)(2,1)S(1)}, bf16[4,32,8,128]{3,2,1,0:T(8,128)(2,1)S(1)}, u32[]{:S(2)}, u32[]{:S(2)}) %collective-permute-start) | collective-permute-done | bytes 262176 | tf_op jit(solution)/shard_map/ppermute | solution.py:15
  30.3 5.9 %collective-permute-done.1 = bf16[4,32,8,128]{3,2,1,0:T(8,128)(2,1)S(1)} collective-permute-done((bf16[4,32,8,128]{3,2,1,0:T(8,128)(2,1)S(1)}, bf16[4,32,8,128]{3,2,1,0:T(8,128)(2,1)S(1)}, u32[]{:S(2)}, u32[]{:S(2)}) %collective-permute-start.1) | collective-permute-done | bytes 262176 | tf_op jit(solution)/shard_map/ppermute | solution.py:15
  36.3 6.3 %fusion.8 = bf16[12,32,8,128]{3,2,1,0:T(8,128)(2,1)S(1)} fusion(bf16[12,32,8,128]{3,2,1,0:T(8,128)(2,1)S(1)} %bitcast.94, bf16[1,12,32,128,128]{4,3,2,1,0:T(8,128)(2,1)} %param.12), kind=kOutput, calls=%fused_computation.12 | convolution fusion | flops 101056512 | bytes 14155776 | tf_op jit(solution)/shard_map/qcfk,qckp->qcfp/dot_general | solution.py:171
  43.3 0.5 fusion.12
  43.9 1.9 %collective-permute-start.2 = (bf16[8,2,512]{2,1,0:T(2,128)(2,1)S(1)}, bf16[8,2,512]{2,1,0:T(2,128)(2,1)S(1)}, u32[]{:S(2)}, u32[]{:S(2)}) collective-permute-start(bf16[8,2,512]{2,1,0:T(2,128)(2,1)S(1)} %get-tuple-element.11), channel_id=1, source_target_pairs={{0,4},{4,8},{8,12},{12,16},{16,20},{20,24},{24,28},{28,32},{32,36}... | collective-permute-start | bytes 49160 | tf_op jit(solution)/shard_map/ppermute | solution.py:25
  45.8 5.8 %collective-permute-start.3 = (bf16[8,2,512]{2,1,0:T(2,128)(2,1)S(1)}, bf16[8,2,512]{2,1,0:T(2,128)(2,1)S(1)}, u32[]{:S(2)}, u32[]{:S(2)}) collective-permute-start(bf16[8,2,512]{2,1,0:T(2,128)(2,1)S(1)} %get-tuple-element.12), channel_id=1, source_target_pairs={{4,0},{8,4},{12,8},{16,12},{20,16},{24,20},{28,24},{32,28},{36,32}... | collective-permute-start | bytes 49160 | tf_op jit(solution)/shard_map/ppermute | solution.py:28
  51.6 1.4 %collective-permute-done.3 = bf16[8,2,512]{2,1,0:T(2,128)(2,1)S(1)} collective-permute-done((bf16[8,2,512]{2,1,0:T(2,128)(2,1)S(1)}, bf16[8,2,512]{2,1,0:T(2,128)(2,1)S(1)}, u32[]{:S(2)}, u32[]{:S(2)}) %collective-permute-start.3) | collective-permute-done | bytes 16416 | tf_op jit(solution)/shard_map/ppermute | solution.py:28
  53.1 0.6 collective-permute-start.4
  53.8 2.7 %collective-permute-start.5 = (bf16[8,68,2]{2,1,0:T(8,128)(2,1)S(1)}, bf16[8,68,2]{2,1,0:T(8,128)(2,1)S(1)}, u32[]{:S(2)}, u32[]{:S(2)}) collective-permute-start(bf16[8,68,2]{2,1,0:T(8,128)(2,1)S(1)} %get-tuple-element.10), channel_id=1, source_target_pairs={{1,0},{2,1},{3,2},{0,3},{5,4},{6,5},{7,6},{4,7},{9,8},{10,9},{11,1... | collective-permute-start | bytes 6536 | tf_op jit(solution)/shard_map/ppermute | solution.py:28
  56.4 0.6 add_convert_fusion.flags
  57.0 2.5 %collective-permute-done.4 = bf16[8,68,2]{2,1,0:T(8,128)(2,1)S(1)} collective-permute-done((bf16[8,68,2]{2,1,0:T(8,128)(2,1)S(1)}, bf16[8,68,2]{2,1,0:T(8,128)(2,1)S(1)}, u32[]{:S(2)}, u32[]{:S(2)}) %collective-permute-start.4) | collective-permute-done | bytes 2208 | tf_op jit(solution)/shard_map/ppermute | solution.py:25
  59.6 0.7 fusion.15
  60.7 1.1 %copy.20.ft = bf16[5,528,128]{2,1,0:T(8,128)(2,1)} copy(bf16[5,528,128]{1,2,0:T(8,128)(2,1)S(1)} %bitcast.96) | data formatting | bytes 1351680 | tf_op jit(solution)/shard_map/reshape | solution.py:186
  61.8 32.3 %conv.1 = bf16[64,512,128]{2,1,0:T(8,128)(2,1)} custom-call(s32[2]{0:T(128)} %add_convert_fusion.flags, bf16[5,528,128]{2,1,0:T(8,128)(2,1)} %copy.20.ft, bf16[72,128]{1,0:T(8,128)(2,1)} %bitcast.107, f32[1,128]{1,0:T(1,128)} %bitcast.108, bf16[9,128,128]{2,1,0:T(8,128)(2,1)} %mw.1, f32[1,128]{1,0:T(1,128)} %bitcast.109), custom_call_target="tpu_custom_call" | custom-call | tf_op jit(solution)/shard_map/conv/pallas_call | solution.py:122
  (43 shorter events, 3.3 us)
Async XLA Ops:
  5.9 16.6 %all-to-all-start = ((bf16[3,4,32,8,128]{4,3,2,0,1:T(8,128)(2,1)}), bf16[3,4,32,8,128]{4,3,2,0,1:T(8,128)(2,1)S(1)}, u32[]{:S(2)}, u32[]{:S(2)}) async-start(bf16[3,4,32,8,128]{4,3,2,0,1:T(8,128)(2,1)} %select_bitcast_fusion.1), calls=%async_computation | async-start | bytes 1572864 | tf_op jit(solution)/shard_map/all_to_all | solution.py:165
  23.2 5.2 %copy-start = (s32[1,12,32]{2,0,1:T(1,128)S(1)}, s32[1,12,32]{2,0,1:T(1,128)}, u32[]{:S(2)}) copy-start(s32[1,12,32]{2,0,1:T(1,128)} %param.13) | copy-start | bytes 4612
  23.4 6.9 %collective-permute-start = (bf16[4,32,8,128]{3,2,1,0:T(8,128)(2,1)S(1)}, bf16[4,32,8,128]{3,2,1,0:T(8,128)(2,1)S(1)}, u32[]{:S(2)}, u32[]{:S(2)}) collective-permute-start(bf16[4,32,8,128]{3,2,1,0:T(8,128)(2,1)S(1)} %get-tuple-element.6), channel_id=1, source_target_pairs={{4,0},{8,4},{12,8},{16,12},{20,16},{24,20},{28,24},{32,28},{36,32}... | collective-permute-start | bytes 786440 | tf_op jit(solution)/shard_map/ppermute | solution.py:15
  26.5 9.8 %collective-permute-start.1 = (bf16[4,32,8,128]{3,2,1,0:T(8,128)(2,1)S(1)}, bf16[4,32,8,128]{3,2,1,0:T(8,128)(2,1)S(1)}, u32[]{:S(2)}, u32[]{:S(2)}) collective-permute-start(bf16[4,32,8,128]{3,2,1,0:T(8,128)(2,1)S(1)} %get-tuple-element.7), channel_id=1, source_target_pairs={{0,4},{4,8},{8,12},{12,16},{16,20},{20,24},{24,28},{28,32},{32,36}... | collective-permute-start | bytes 786440 | tf_op jit(solution)/shard_map/ppermute | solution.py:15
  43.9 7.7 %collective-permute-start.2 = (bf16[8,2,512]{2,1,0:T(2,128)(2,1)S(1)}, bf16[8,2,512]{2,1,0:T(2,128)(2,1)S(1)}, u32[]{:S(2)}, u32[]{:S(2)}) collective-permute-start(bf16[8,2,512]{2,1,0:T(2,128)(2,1)S(1)} %get-tuple-element.11), channel_id=1, source_target_pairs={{0,4},{4,8},{8,12},{12,16},{16,20},{20,24},{24,28},{28,32},{32,36}... | collective-permute-start | bytes 49160 | tf_op jit(solution)/shard_map/ppermute | solution.py:25
  45.8 7.2 %collective-permute-start.3 = (bf16[8,2,512]{2,1,0:T(2,128)(2,1)S(1)}, bf16[8,2,512]{2,1,0:T(2,128)(2,1)S(1)}, u32[]{:S(2)}, u32[]{:S(2)}) collective-permute-start(bf16[8,2,512]{2,1,0:T(2,128)(2,1)S(1)} %get-tuple-element.12), channel_id=1, source_target_pairs={{4,0},{8,4},{12,8},{16,12},{20,16},{24,20},{28,24},{32,28},{36,32}... | collective-permute-start | bytes 49160 | tf_op jit(solution)/shard_map/ppermute | solution.py:28
  53.1 6.4 %collective-permute-start.4 = (bf16[8,68,2]{2,1,0:T(8,128)(2,1)S(1)}, bf16[8,68,2]{2,1,0:T(8,128)(2,1)S(1)}, u32[]{:S(2)}, u32[]{:S(2)}) collective-permute-start(bf16[8,68,2]{2,1,0:T(8,128)(2,1)S(1)} %get-tuple-element.9), channel_id=1, source_target_pairs={{0,1},{1,2},{2,3},{3,0},{4,5},{5,6},{6,7},{7,4},{8,9},{9,10},{10,1... | collective-permute-start | bytes 6536 | tf_op jit(solution)/shard_map/ppermute | solution.py:25
  53.8 5.8 %collective-permute-start.5 = (bf16[8,68,2]{2,1,0:T(8,128)(2,1)S(1)}, bf16[8,68,2]{2,1,0:T(8,128)(2,1)S(1)}, u32[]{:S(2)}, u32[]{:S(2)}) collective-permute-start(bf16[8,68,2]{2,1,0:T(8,128)(2,1)S(1)} %get-tuple-element.10), channel_id=1, source_target_pairs={{1,0},{2,1},{3,2},{0,3},{5,4},{6,5},{7,6},{4,7},{9,8},{10,9},{11,1... | collective-permute-start | bytes 6536 | tf_op jit(solution)/shard_map/ppermute | solution.py:28

commit v2 on v1

--- a/solution.py
+++ b/solution.py
@@ -5,29 +5,276 @@
 from jax.experimental.pallas import tpu as pltpu
 from jax.sharding import PartitionSpec as P
 
-ROWS_DEV = 64
-COLS_DEV = 512
-
-
-def shifted(block, axis, distance):
-    devices = range(lax.axis_size(axis))
-    route = [(i - distance, i) for i in devices if i - distance in devices]
-    return lax.ppermute(block, axis, route)
-
-
-def extended(block, sides, width, periodic):
-    for axis, dim in sides:
-        count = lax.axis_size(axis)
-        forward = [(i, i + 1) for i in range(count - 1)]
-        if periodic:
-            forward.append((count - 1, 0))
-        backward = [(target, source) for source, target in forward]
-        low = lax.ppermute(
-            lax.slice_in_dim(block, block.shape[dim] - width, None, axis=dim), axis, forward
+NT = (((1,), (1,)), ((), ()))
+
+
+def gather_kernel(src, routes, window, weights, ft, wv, s32, o32, sendb, recvb, c32, place, fs32, fe, colr, coll,
+                  lc, ln, ls, rc, rn, rs, w_sem, send_sem, recv_sem, hs_sem, hr_sem):
+    f32, bf16 = jnp.float32, jnp.bfloat16
+    n_band, n_lon = lax.axis_size("band"), lax.axis_size("lon")
+    band, lon = lax.axis_index("band"), lax.axis_index("lon")
+    barrier = pltpu.get_barrier_semaphore()
+
+    def there(q):
+        return {"band": band + (q // 4 - 1), "lon": lax.rem(lon + q % 4, n_lon)}
+
+    def inside(b):
+        return jnp.logical_and(b >= 0, b < n_band)
+
+    def edge(b):
+        return jnp.logical_or(b == 0, b == n_band - 1)
+
+    def sends(q):
+        ok = inside(band + (q // 4 - 1))
+        return jnp.logical_and(ok, edge(band)) if q % 4 == 2 else ok
+
+    def gets(q):
+        origin = band - (q // 4 - 1)
+        return jnp.logical_and(inside(origin), edge(origin)) if q % 4 == 2 else inside(origin)
+
+    def greets(q):
+        target = band + (q // 4 - 1)
+        ok = inside(target)
+        return jnp.logical_and(ok, jnp.logical_or(edge(band), edge(target))) if q % 4 == 2 else ok
+
+    others = [q for q in range(12) if q != 4]
+    count = jnp.int32(0)
+    for q in others:
+        @pl.when(greets(q))
+        def _():
+            pl.semaphore_signal(barrier, inc=1, device_id=there(q), device_id_type=pl.DeviceIdType.MESH)
+        count = count + greets(q).astype(jnp.int32)
+
+    order = (4, 0, 8, 5, 7, 1, 3, 9, 11, 6, 2, 10)
+
+    def fetch(q):
+        return pltpu.make_async_copy(weights.at[q], wv.at[q], w_sem.at[q])
+
+    for q in order:
+        fetch(q).start()
+
+    code = lax.broadcasted_iota(jnp.int32, (128, 128), 1)
+    block = lax.broadcasted_iota(jnp.int32, (128, 128), 0)
+    names = jnp.logical_or(routes[:, 0:1] == code, routes[:, 1:2] == code)
+    earlier = (code < block).astype(f32).astype(bf16)
+    rank = jnp.dot(earlier, names.astype(f32).astype(bf16), preferred_element_type=f32)
+    ranked = jnp.where(names, rank, -1.0).T
+    slot = lax.broadcasted_iota(jnp.int32, (32, 128), 0).astype(f32)
+    select = jnp.concatenate(
+        [(jnp.broadcast_to(ranked[q : q + 1], (32, 128)) == slot).astype(f32) for q in range(12)], axis=0
+    ).astype(bf16)
+    s32[...] = src[...].astype(f32).reshape(1024, 128)
+    for f in range(0, 8, 2):
+        planes = jnp.concatenate(
+            [s32[pl.ds(f + i, 128, stride=8), :].astype(bf16) for i in range(2)], axis=1
         )
-        high = lax.ppermute(lax.slice_in_dim(block, 0, width, axis=dim), axis, backward)
-        block = jnp.concatenate([low, block, high], axis=dim)
-    return block
+        packed = jnp.dot(select, planes, preferred_element_type=f32)
+        for i in range(2):
+            o32[pl.ds(f + i, 384, stride=8), :] = packed[:, i * 128 : i * 128 + 128]
+    for q in range(12):
+        sendb[q] = o32[q * 256 : q * 256 + 256, :].astype(bf16)
+
+    pl.semaphore_wait(barrier, count)
+
+    def route(q):
+        return pltpu.make_async_remote_copy(
+            src_ref=sendb.at[q], dst_ref=recvb.at[q], send_sem=send_sem.at[q], recv_sem=recv_sem.at[q],
+            device_id=there(q), device_id_type=pl.DeviceIdType.MESH,
+        )
+
+    for q in (2, 6, 10, 1, 3, 9, 11, 5, 7, 0, 8):
+        @pl.when(sends(q))
+        def _():
+            route(q).start()
+
+    spot = lax.broadcasted_iota(jnp.int32, (256, 384), 0)
+    wanted = lax.rem(spot, 64) * 4 + lax.div(spot, 64)
+    place[...] = (jnp.broadcast_to(window[...], (256, 384)) == wanted).astype(f32).astype(bf16)
+    zero_rows = jnp.zeros((16, 512), bf16)
+    zero_tile = jnp.zeros((16, 128), bf16)
+    fe[544:576, :] = jnp.zeros((32, 512), bf16)
+
+    @pl.when(band == 0)
+    def _():
+        fe[0:16, :] = zero_rows
+        ln[...] = zero_tile
+        rn[...] = zero_tile
+
+    @pl.when(band == n_band - 1)
+    def _():
+        fe[528:544, :] = zero_rows
+        ls[...] = zero_tile
+        rs[...] = zero_tile
+
+    for q in order:
+        if q == 4:
+            held = sendb.at[4]
+        else:
+            held = recvb.at[q]
+
+            @pl.when(gets(q))
+            def _():
+                route(q).wait_recv()
+
+            @pl.when(jnp.logical_not(gets(q)))
+            def _():
+                recvb[q] = jnp.zeros((256, 128), bf16)
+
+        fetch(q).wait()
+
+        def group(g, carry):
+            for i in range(8):
+                row = pl.multiple_of((g * 8 + i) * 16, 16)
+                col = pl.multiple_of((g * 8 + i) * 256, 256)
+                both = jnp.concatenate([wv[q, pl.ds(col, 128), :], wv[q, pl.ds(col + 128, 128), :]], axis=1)
+                got = jnp.dot(held[pl.ds(row, 16), :], both, preferred_element_type=f32)
+                c32[pl.ds(q * 256 + row, 8), :] = got[0:8, 0:128]
+                c32[pl.ds(q * 256 + row + 8, 8), :] = got[8:16, 128:256]
+            return carry
+
+        lax.fori_loop(0, 2, group, 0)
+
+    for f in range(0, 8, 2):
+        planes = jnp.concatenate(
+            [c32[pl.ds(f + i, 384, stride=8), :].astype(bf16) for i in range(2)], axis=1
+        )
+        summed = jnp.dot(place[...], planes, preferred_element_type=f32)
+        for i in range(2):
+            for c in range(4):
+                fs32[c, pl.ds(f + i, 64, stride=8), :] = summed[
+                    c * 64 : c * 64 + 64, i * 128 : i * 128 + 128
+                ]
+    for c in range(4):
+        fe[16:528, c * 128 : c * 128 + 128] = fs32[c].astype(bf16)
+
+    pick_row = lax.broadcasted_iota(jnp.int32, (16, 128), 0)
+    pick_col = lax.broadcasted_iota(jnp.int32, (16, 128), 1)
+    pick_left = jnp.logical_and(pick_row == pick_col, pick_row < 2).astype(f32).astype(bf16)
+    pick_right = (pick_col == pick_row + 112).astype(f32)
+    pick_right = jnp.where(pick_row >= 14, pick_right, 0.0).astype(bf16)
+    coll[...] = lax.dot_general(pick_left, fe[16:528, 0:128], NT, preferred_element_type=f32).astype(bf16)
+    colr[...] = lax.dot_general(pick_right, fe[16:528, 384:512], NT, preferred_element_type=f32).astype(bf16)
+
+    east, west = lax.rem(lon + 1, n_lon), lax.rem(lon + n_lon - 1, n_lon)
+    north, south = band - 1, band + 1
+
+    def halo(i, source, target, b, l):
+        return pltpu.make_async_remote_copy(
+            src_ref=source, dst_ref=target, send_sem=hs_sem.at[i], recv_sem=hr_sem.at[i],
+            device_id={"band": b, "lon": l}, device_id_type=pl.DeviceIdType.MESH,
+        )
+
+    up = [
+        halo(0, colr.at[:, 0:128], ls, north, east),
+        halo(1, coll.at[:, 0:128], rs, north, west),
+        halo(2, fe.at[16:32, :], fe.at[528:544, :], north, lon),
+    ]
+    down = [
+        halo(3, colr.at[:, 384:512], ln, south, east),
+        halo(4, coll.at[:, 384:512], rn, south, west),
+        halo(5, fe.at[512:528, :], fe.at[0:16, :], south, lon),
+    ]
+    side = [halo(6, colr, lc, band, east), halo(7, coll, rc, band, west)]
+
+    @pl.when(band > 0)
+    def _():
+        for c in up:
+            c.start()
+
+    @pl.when(band < n_band - 1)
+    def _():
+        for c in down:
+            c.start()
+
+    for c in side:
+        c.start()
+
+    same = (lax.broadcasted_iota(jnp.int32, (128, 128), 0) == lax.broadcasted_iota(jnp.int32, (128, 128), 1))
+    same = same.astype(f32).astype(bf16)
+
+    def turn(k):
+        for t in range(4):
+            ft[k, 16 + t * 128 : 144 + t * 128, :] = lax.dot_general(
+                same, fe[112 * k : 112 * k + 128, t * 128 : t * 128 + 128], NT, preferred_element_type=f32
+            ).astype(bf16)
+
+    for k in (1, 2, 3):
+        turn(k)
+
+    @pl.when(band < n_band - 1)
+    def _():
+        for c in up:
+            c.wait_recv()
+
+    @pl.when(band > 0)
+    def _():
+        for c in down:
+            c.wait_recv()
+
+    for c in side:
+        c.wait_recv()
+    for k in (0, 4):
+        turn(k)
+
+    lane = lax.broadcasted_iota(jnp.int32, (16, 640), 1)
+    blank = jnp.zeros((16, 512), f32)
+
+    def column(c, n, s):
+        mid = pltpu.roll(jnp.concatenate([c[...].astype(f32), jnp.zeros((16, 128), f32)], axis=1), 16, 1)
+        top = jnp.concatenate([pltpu.roll(n[...].astype(f32), 16, 1), blank], axis=1)
+        low = jnp.concatenate([blank, pltpu.roll(s[...].astype(f32), 16, 1)], axis=1)
+        whole = jnp.where(lane < 16, top, jnp.where(lane < 528, mid, jnp.where(lane < 544, low, 0.0)))
+        return [
+            (whole if k == 0 else pltpu.roll(whole, 640 - 112 * k, 1))[:, 0:128].astype(bf16) for k in range(5)
+        ]
+
+    left, right = column(lc, ln, ls), column(rc, rn, rs)
+    for k in range(5):
+        ft[k, 0:16, :] = left[k]
+        ft[k, 528:544, :] = right[k]
+
+    for q in others:
+        @pl.when(sends(q))
+        def _():
+            route(q).wait_send()
+
+    @pl.when(band > 0)
+    def _():
+        for c in up:
+            c.wait_send()
+
+    @pl.when(band < n_band - 1)
+    def _():
+        for c in down:
+            c.wait_send()
+
+    for c in side:
+        c.wait_send()
+
+
+def gather(source, routes, window, weights):
+    V, D = pltpu.VMEM, pltpu.SemaphoreType.DMA
+    bf16, f32 = jnp.bfloat16, jnp.float32
+    vm = pl.BlockSpec(memory_space=pltpu.VMEM)
+    return pl.pallas_call(
+        gather_kernel,
+        out_shape=jax.ShapeDtypeStruct((5, 544, 128), bf16),
+        in_specs=[vm, vm, vm, pl.BlockSpec(memory_space=pl.ANY)],
+        out_specs=vm,
+        scratch_shapes=[
+            V((12, 4096, 128), bf16), V((1024, 128), f32), V((3072, 128), f32),
+            V((12, 256, 128), bf16), V((12, 256, 128), bf16), V((3072, 128), f32),
+            V((256, 384), bf16), V((4, 512, 128), f32), V((576, 512), bf16),
+            V((16, 512), bf16), V((16, 512), bf16),
+            V((16, 512), bf16), V((16, 128), bf16), V((16, 128), bf16),
+            V((16, 512), bf16), V((16, 128), bf16), V((16, 128), bf16),
+            D((12,)), D((12,)), D((12,)), D((8,)), D((8,)),
+        ],
+        compiler_params=pltpu.CompilerParams(
+            collective_id=0, has_side_effects=True, vmem_limit_bytes=56 * 1024 * 1024
+        ),
+        name="gather",
+    )(source, routes, window, weights)
 
 
 MCH = 256
@@ -56,7 +303,7 @@
     for k in range(5):
         tmp[...] = ft[k].astype(f32)
         for b in range(3):
-            lhs3[k, :, b * 128 : b * 128 + 128] = tmp[b : b + 520].astype(bf16)
+            lhs3[k, :, b * 128 : b * 128 + 128] = tmp[b + 14 : b + 534].astype(bf16)
 
     hb = sb[...] * 0.5
     bias = mb[...]
@@ -126,7 +373,7 @@
         out_specs=pl.BlockSpec(memory_space=pl.ANY),
         scratch_shapes=[
             V((7, 384, 256), bf16), V((1536, 256), bf16), V((5, 520, 384), bf16),
-            V((528, 128), f32), V((2, 520, 128), f32),
+            V((544, 128), f32), V((2, 520, 128), f32),
             V((2, 512, 384), bf16), V((2, 512, 384), bf16), V((2, 512, 384), bf16),
             V((2, 512, 128), bf16), V((2, 512, 128), bf16), V((2, 512, 128), bf16),
             pltpu.SemaphoreType.DMA((3,)),
@@ -137,55 +384,9 @@
 
 
 def on_device(source, routes, slot_weights, window, stem_weight, stem_bias, mix_weight, mix_bias):
-    n_lon = lax.axis_size("lon")
-    lon_here = lax.axis_index("lon")
-    blk_dev, fields, cells = source.shape
-    nbr = slot_weights.shape[1]
-    cap = slot_weights.shape[2]
-    pixels = slot_weights.shape[4]
-    top = routes.shape[1]
-    rows = ROWS_DEV
-    cols = COLS_DEV
-    nwin = rows * cols // pixels
-    flat_dest = routes.reshape(-1)
-    onehot = (flat_dest[:, None] == jnp.arange(nbr, dtype=jnp.int32)[None, :]).astype(jnp.int32)
-    before = jnp.cumsum(onehot, axis=0) - onehot
-    rank = jnp.sum(before * onehot, axis=1)
-    target_slot = flat_dest * cap + rank
-    select = (jnp.arange(nbr * cap, dtype=jnp.int32)[:, None] == target_slot[None, :]).astype(
-        jnp.bfloat16
-    )
-    repeated = jnp.repeat(source.reshape(blk_dev, fields * cells), top, axis=0)
-    outgoing = jnp.dot(select, repeated, preferred_element_type=jnp.float32).astype(jnp.bfloat16)
-    outgoing = outgoing.reshape(3, n_lon, cap, fields, cells)
-    lanes = jnp.arange(n_lon, dtype=jnp.int32)
-    to_absolute = (lanes - lon_here) % n_lon
-    to_relative = (lon_here - lanes) % n_lon
-    absolute = jnp.take(outgoing, to_absolute, axis=1)
-    arrived = lax.all_to_all(absolute, "lon", split_axis=1, concat_axis=1, tiled=True)
-    arrived = jnp.take(arrived, to_relative, axis=1)
-    from_north = shifted(arrived[0], "band", -1)
-    from_south = shifted(arrived[2], "band", 1)
-    incoming = jnp.stack([from_north, arrived[1], from_south], axis=0)
-    incoming = incoming.reshape(nbr, cap, fields, cells)
-    contrib = jnp.einsum(
-        "qcfk,qckp->qcfp", incoming, slot_weights[0], preferred_element_type=jnp.float32
-    ).astype(jnp.bfloat16)
-    place = (jnp.arange(nwin, dtype=jnp.int32)[:, None] == window[0].reshape(-1)[None, :]).astype(
-        jnp.bfloat16
-    )
-    summed = jnp.dot(
-        place, contrib.reshape(nbr * cap, fields * pixels), preferred_element_type=jnp.float32
-    )
-    field = summed.reshape(rows, cols // pixels, fields, pixels).transpose(2, 0, 1, 3)
-    field = field.reshape(fields, rows, cols).astype(jnp.bfloat16)
-    with_rows = extended(field, (("band", 1),), 2, False)
-    full = extended(with_rows, (("lon", 2),), 2, True)
-    full = jnp.pad(full, ((0, 0), (0, 4), (0, 12)))
-    windows = jnp.stack([full[:, 14 * k : 14 * k + 16] for k in range(5)], axis=0)
-    windows = windows.transpose(0, 3, 2, 1).reshape(5, cols + 16, 16 * fields)
     band = lax.axis_index("band")
     flags = jnp.stack([band == 0, band == lax.axis_size("band") - 1]).astype(jnp.int32)
+    windows = gather(source, routes, window.reshape(1, 384), slot_weights.reshape(12, 4096, 128))
     return conv(
         flags,
         windows,

time: 95.1 us -> 57.3 us (0.60)
  waiting for transfers between devices: 23.9 us -> 0 us
  Pallas kernels: 32.3 us -> 53.7 us
  starting transfers between devices: 20.3 us -> 0 us
  matrix products: 7.21 us -> 0 us
  local copies, waits for them, and re-layouts: 6.62 us -> 2.06 us
  other arithmetic: 3.54 us -> 1.33 us
    pallas_call x0 -> x1, Pallas kernels: none -> 21.4 us  [gather(): pl.pallas_call(gather_kernel, out_shape=jax.ShapeDtypeStruct((5, 544, 128...]
    ppermute x6 -> x0, starting transfers between devices: 16 us -> none  [the longest x2 8.42 us: extended(): lax.ppermute(lax.slice_in_dim(block, 0, width, axis=dim), axis, backward)]
    all_to_all x1 -> x0, waiting for transfers between devices: 12.2 us -> none  [on_device(): lax.all_to_all(absolute, 'lon', split_axis=1, concat_axis=1, tiled=True)]
    ppermute x6 -> x0, waiting for transfers between devices: 11.7 us -> none  [the longest x2 7.75 us: shifted(): return lax.ppermute(block, axis, route)]
    dot_general x3 -> x0, matrix products: 7.21 us -> none  [the longest x1 6.35 us: on_device(): jnp.einsum('qcfk,qckp->qcfp', incoming, slot_weights[0], preferred_elemen...]
    all_to_all x1 -> x0, starting transfers between devices: 4.29 us -> none  [on_device(): lax.all_to_all(absolute, 'lon', split_axis=1, concat_axis=1, tiled=True)]
    gather x2 -> x0, local copies, waits for them, and re-layouts: 1.4 us -> none  [the longest x1 0.7 us: on_device(): absolute = jnp.take(outgoing, to_absolute, axis=1)]
    select_n x4 -> x0, other arithmetic: 1.18 us -> none  [the longest x2 1.03 us: on_device(): absolute = jnp.take(outgoing, to_absolute, axis=1)]
  transfers between devices with their start and end apart: 7 -> 0, of which waited for: 5 -> 0; matrix products, arithmetic and copies ran while one was open for 1% -> 0% of each run, Pallas kernels for 0% -> 0%
where the time goes in v2:
time: 57.3 us; the launch traced here: 57.1 us
  Pallas kernels  53.7 us (94%)
  local copies, waits for them, and re-layouts  2.06 us (4%)
  other arithmetic  1.33 us (2%)
    pallas_call x1, Pallas kernels, conv(): pl.pallas_call(conv_kernel, out_shape=jax.ShapeDtypeStruct((64, 512, 128)...  32.3 us
    pallas_call x1, Pallas kernels, gather(): pl.pallas_call(gather_kernel, out_shape=jax.ShapeDtypeStruct((5, 544, 128...  21.4 us
    unnamed x1, local copies, waits for them, and re-layouts  1.41 us

profile of v2, /device:TPU:96, one launch (start us, length us, event | category | flops | bytes accessed | tf_op | source)
XLA Modules:
  0.0 57.1 jit_solution(13997106520948866165)
XLA Ops:
  0.0 0.6 %add_convert_fusion.flags = s32[2]{0:T(128)} fusion(pred[1]{0:T(512)(128)(4,1)} %bitcast.1, pred[1]{0:T(512)(128)(4,1)} %bitcast), kind=kLoop, calls=%fused_computation | loop fusion | flops 4 | bytes 10 | tf_op jit(solution)/shard_map/convert_element_type | solution.py:388
  0.6 0.7 %reduce = s32[12,32]{1,0:T(8,128)S(1)} reduce(s32[1,12,32]{2,0,1:T(1,128)} %param.11, s32[]{:T(128)} %constant.8.clone.1), dimensions={0}, to_apply=%param.11.reduce_sub_computation | reduce | bytes 3076 | tf_op args[3]
  1.3 0.7 %reshape.15.window = s32[1,384]{1,0:T(1,128)} reshape(s32[12,32]{1,0:T(8,128)S(1)} %reduce) | data formatting | bytes 3072 | tf_op jit(solution)/shard_map/reshape | solution.py:389
  2.0 1.4 %copy.9.routes = s32[128,2]{1,0:T(8,128)} copy(s32[128,2]{0,1:T(2,128)} %param.9) | data formatting | bytes 2048 | tf_op args[1]
  3.4 21.4 %gather.1.ft = bf16[5,544,128]{2,1,0:T(8,128)(2,1)} custom-call(bf16[128,8,128]{2,1,0:T(8,128)(2,1)} %src.1, s32[128,2]{1,0:T(8,128)} %copy.9.routes, s32[1,384]{1,0:T(1,128)} %reshape.15.window, bf16[12,4096,128]{2,1,0:T(8,128)(2,1)} %bitcast.6), custom_call_target="tpu_custom_call" | custom-call | tf_op jit(solution)/shard_map/gather/pallas_call | solution.py:259
  24.8 32.3 %conv.1 = bf16[64,512,128]{2,1,0:T(8,128)(2,1)} custom-call(s32[2]{0:T(128)} %add_convert_fusion.flags, bf16[5,544,128]{2,1,0:T(8,128)(2,1)} %gather.1.ft, bf16[72,128]{1,0:T(8,128)(2,1)} %bitcast.7, f32[1,128]{1,0:T(1,128)} %bitcast.8, bf16[9,128,128]{2,1,0:T(8,128)(2,1)} %mw.1, f32[1,128]{1,0:T(1,128)} %bitcast.9), custom_call_target="tpu_custom_call" | custom-call | tf_op jit(solution)/shard_map/conv/pallas_call | solution.py:369

commit v3 on v2

v3 whole, which is shorter than its diff:
```python
import jax
import jax.numpy as jnp
from jax import lax
from jax.experimental import pallas as pl
from jax.experimental.pallas import tpu as pltpu
from jax.sharding import PartitionSpec as P

NT = (((1,), (1,)), ((), ()))


def gather_kernel(src, routes, window, weights, out, wv, s32, o32, sendb, recvb, c32, place, fs32, fe, colr, coll,
                  lc, ln, ls, rc, rn, rs, y32, lv, w_sem, send_sem, recv_sem, hs_sem, hr_sem, o_sem, e_sem):
    f32, bf16 = jnp.float32, jnp.bfloat16
    n_band, n_lon = lax.axis_size("band"), lax.axis_size("lon")
    band, lon = lax.axis_index("band"), lax.axis_index("lon")
    barrier = pltpu.get_barrier_semaphore()

    def there(q):
        return {"band": band + (q // 4 - 1), "lon": lax.rem(lon + q % 4, n_lon)}

    def inside(b):
        return jnp.logical_and(b >= 0, b < n_band)

    def edge(b):
        return jnp.logical_or(b == 0, b == n_band - 1)

    def sends(q):
        ok = inside(band + (q // 4 - 1))
        return jnp.logical_and(ok, edge(band)) if q % 4 == 2 else ok

    def gets(q):
        origin = band - (q // 4 - 1)
        return jnp.logical_and(inside(origin), edge(origin)) if q % 4 == 2 else inside(origin)

    def greets(q):
        target = band + (q // 4 - 1)
        ok = inside(target)
        return jnp.logical_and(ok, jnp.logical_or(edge(band), edge(target))) if q % 4 == 2 else ok

    others = [q for q in range(12) if q != 4]
    count = jnp.int32(0)
    for q in others:
        @pl.when(greets(q))
        def _():
            pl.semaphore_signal(barrier, inc=1, device_id=there(q), device_id_type=pl.DeviceIdType.MESH)
        count = count + greets(q).astype(jnp.int32)

    order = (4, 0, 8, 5, 7, 1, 3, 9, 11, 6, 2, 10)

    def fetch(q):
        return pltpu.make_async_copy(weights.at[q], wv.at[q], w_sem.at[q])

    for q in order:
        fetch(q).start()

    code = lax.broadcasted_iota(jnp.int32, (16, 128), 0)
    names = jnp.logical_or(routes[0:1, :] == code, routes[1:2, :] == code)
    earlier = lax.broadcasted_iota(jnp.int32, (128, 128), 0) < lax.broadcasted_iota(jnp.int32, (128, 128), 1)
    rank = jnp.dot(
        names.astype(f32).astype(bf16), earlier.astype(f32).astype(bf16), preferred_element_type=f32
    )
    ranked = jnp.where(names, rank, -1.0)
    slot = lax.broadcasted_iota(jnp.int32, (32, 128), 0).astype(f32)
    select = jnp.concatenate(
        [(jnp.broadcast_to(ranked[q : q + 1], (32, 128)) == slot).astype(f32) for q in range(12)], axis=0
    ).astype(bf16)
    s32[...] = src[...].astype(f32).reshape(1024, 128)
    for f in range(0, 8, 2):
        planes = jnp.concatenate(
            [s32[pl.ds(f + i, 128, stride=8), :].astype(bf16) for i in range(2)], axis=1
        )
        packed = jnp.dot(select, planes, preferred_element_type=f32)
        for i in range(2):
            o32[pl.ds(f + i, 384, stride=8), :] = packed[:, i * 128 : i * 128 + 128]
    for q in range(12):
        sendb[q] = o32[q * 256 : q * 256 + 256, :].astype(bf16)

    pl.semaphore_wait(barrier, count)

    def route(q):
        return pltpu.make_async_remote_copy(
            src_ref=sendb.at[q], dst_ref=recvb.at[q], send_sem=send_sem.at[q], recv_sem=recv_sem.at[q],
            device_id=there(q), device_id_type=pl.DeviceIdType.MESH,
        )

    for q in (2, 6, 10, 1, 3, 9, 11, 5, 7, 0, 8):
        @pl.when(sends(q))
        def _():
            route(q).start()

    spot = lax.broadcasted_iota(jnp.int32, (256, 384), 0)
    wanted = lax.rem(spot, 64) * 4 + lax.div(spot, 64)
    lands = jnp.concatenate([window[q] for q in range(12)], axis=1)
    place[...] = (jnp.broadcast_to(lands, (256, 384)) == wanted).astype(f32).astype(bf16)
    zero_rows = jnp.zeros((16, 512), bf16)
    zero_tile = jnp.zeros((16, 128), bf16)
    fe[544:592, :] = jnp.zeros((48, 512), bf16)

    @pl.when(band == 0)
    def _():
        fe[0:16, :] = zero_rows
        ln[...] = zero_tile
        rn[...] = zero_tile

    @pl.when(band == n_band - 1)
    def _():
        fe[528:544, :] = zero_rows
        ls[...] = zero_tile
        rs[...] = zero_tile

    for q in order:
        if q == 4:
            held = sendb.at[4]
        else:
            held = recvb.at[q]

            @pl.when(gets(q))
            def _():
                route(q).wait_recv()

            @pl.when(jnp.logical_not(gets(q)))
            def _():
                recvb[q] = jnp.zeros((256, 128), bf16)

        fetch(q).wait()

        for i in range(16):
            col = i * 256
            both = jnp.concatenate([wv[q, col : col + 128, :], wv[q, col + 128 : col + 256, :]], axis=1)
            got = jnp.dot(held[i * 16 : i * 16 + 16, :], both, preferred_element_type=f32)
            c32[q * 256 + i * 16 : q * 256 + i * 16 + 8, :] = got[0:8, 0:128]
            c32[q * 256 + i * 16 + 8 : q * 256 + i * 16 + 16, :] = got[8:16, 128:256]

    for f in range(0, 8, 2):
        planes = jnp.concatenate(
            [c32[pl.ds(f + i, 384, stride=8), :].astype(bf16) for i in range(2)], axis=1
        )
        summed = jnp.dot(place[...], planes, preferred_element_type=f32)
        for i in range(2):
            for c in range(4):
                fs32[c, pl.ds(f + i, 64, stride=8), :] = summed[
                    c * 64 : c * 64 + 64, i * 128 : i * 128 + 128
                ]
    for c in range(4):
        fe[16:528, c * 128 : c * 128 + 128] = fs32[c].astype(bf16)

    pick_row = lax.broadcasted_iota(jnp.int32, (16, 128), 0)
    pick_col = lax.broadcasted_iota(jnp.int32, (16, 128), 1)
    pick_left = jnp.logical_and(pick_row == pick_col, pick_row < 2).astype(f32).astype(bf16)
    pick_right = (pick_col == pick_row + 112).astype(f32)
    pick_right = jnp.where(pick_row >= 14, pick_right, 0.0).astype(bf16)
    coll[...] = lax.dot_general(pick_left, fe[16:528, 0:128], NT, preferred_element_type=f32).astype(bf16)
    colr[...] = lax.dot_general(pick_right, fe[16:528, 384:512], NT, preferred_element_type=f32).astype(bf16)

    east, west = lax.rem(lon + 1, n_lon), lax.rem(lon + n_lon - 1, n_lon)
    north, south = band - 1, band + 1

    def halo(i, source, target, b, l):
        return pltpu.make_async_remote_copy(
            src_ref=source, dst_ref=target, send_sem=hs_sem.at[i], recv_sem=hr_sem.at[i],
            device_id={"band": b, "lon": l}, device_id_type=pl.DeviceIdType.MESH,
        )

    up = [
        halo(0, colr.at[:, 0:128], ls, north, east),
        halo(1, coll.at[:, 0:128], rs, north, west),
        halo(2, fe.at[16:32, :], fe.at[528:544, :], north, lon),
    ]
    down = [
        halo(3, colr.at[:, 384:512], ln, south, east),
        halo(4, coll.at[:, 384:512], rn, south, west),
        halo(5, fe.at[512:528, :], fe.at[0:16, :], south, lon),
    ]
    side = [halo(6, colr, lc, band, east), halo(7, coll, rc, band, west)]

    @pl.when(band > 0)
    def _():
        for c in up:
            c.start()

    @pl.when(band < n_band - 1)
    def _():
        for c in down:
            c.start()

    for c in side:
        c.start()

    same = (lax.broadcasted_iota(jnp.int32, (128, 128), 0) == lax.broadcasted_iota(jnp.int32, (128, 128), 1))
    same = same.astype(f32).astype(bf16)
    pad = jnp.zeros((16, 128), bf16)

    def turn(w):
        for t in range(4):
            piece = fe[64 * w : 64 * w + 80, t * 128 : t * 128 + 128]
            turned = lax.dot_general(
                same, jnp.concatenate([piece, piece, piece, pad], axis=0), NT, preferred_element_type=f32
            )
            for i in range(2):
                y32[w, i, 16 + t * 128 : 144 + t * 128, :] = turned[:, i * 128 : i * 128 + 128]

    def shift(w, start, size):
        lane = lax.broadcasted_iota(jnp.int32, (size, 128), 1)
        at = [slice(start + 14 + b, start + 14 + b + size) for b in range(3)]
        low = jnp.where(lane < 80, y32[w, 0, at[0], :], y32[w, 0, at[1], :])
        high = jnp.where(lane < 32, y32[w, 1, at[1], :], y32[w, 1, at[2], :])
        lv[w, start : start + size, 0:128] = low.astype(bf16)
        lv[w, start : start + size, 128:256] = high.astype(bf16)

    def body_out(w):
        return pltpu.make_async_copy(lv.at[w, 16:496, :], out.at[w, 16:496, :], o_sem.at[w])

    def ends_out(i):
        part = (slice(0, 16), slice(496, 528))[i]
        return pltpu.make_async_copy(lv.at[:, part, :], out.at[:, part, :], e_sem.at[i])

    for w in range(1, 8):
        turn(w)
        shift(w, 16, 480)
        body_out(w).start()

    @pl.when(band < n_band - 1)
    def _():
        for c in up:
            c.wait_recv()

    @pl.when(band > 0)
    def _():
        for c in down:
            c.wait_recv()

    for c in side:
        c.wait_recv()
    for w in (0, 8):
        turn(w)
        shift(w, 16, 480)
        body_out(w).start()

    lane = lax.broadcasted_iota(jnp.int32, (16, 640), 1)
    blank = jnp.zeros((16, 512), f32)
    mid = lc[...].astype(f32) + rc[...].astype(f32)
    mid = pltpu.roll(jnp.concatenate([mid, jnp.zeros((16, 128), f32)], axis=1), 16, 1)
    top = jnp.concatenate([pltpu.roll(ln[...].astype(f32) + rn[...].astype(f32), 16, 1), blank], axis=1)
    low = jnp.concatenate([blank, pltpu.roll(ls[...].astype(f32) + rs[...].astype(f32), 16, 1)], axis=1)
    whole = jnp.where(lane < 16, top, jnp.where(lane < 528, mid, jnp.where(lane < 544, low, 0.0)))
    lane = lax.broadcasted_iota(jnp.int32, (16, 256), 1)
    for w in range(9):
        first = (whole if w == 0 else pltpu.roll(whole, 640 - 64 * w, 1))[:, 0:256]
        first = jnp.where(lane < 80, first, 0.0)
        first = first + pltpu.roll(first, 80, 1) + pltpu.roll(first, 160, 1)
        for i in range(2):
            y32[w, i, 0:16, :] = first[:, i * 128 : i * 128 + 128]
            y32[w, i, 528:544, :] = first[:, i * 128 : i * 128 + 128]
        shift(w, 0, 16)
        shift(w, 496, 32)
    for i in range(2):
        ends_out(i).start()
    for w in range(9):
        body_out(w).wait()
    for i in range(2):
        ends_out(i).wait()

    for q in others:
        @pl.when(sends(q))
        def _():
            route(q).wait_send()

    @pl.when(band > 0)
    def _():
        for c in up:
            c.wait_send()

    @pl.when(band < n_band - 1)
    def _():
        for c in down:
            c.wait_send()

    for c in side:
        c.wait_send()


def gather(source, routes, window, weights):
    V, D = pltpu.VMEM, pltpu.SemaphoreType.DMA
    bf16, f32 = jnp.bfloat16, jnp.float32
    vm = pl.BlockSpec(memory_space=pltpu.VMEM)
    return pl.pallas_call(
        gather_kernel,
        out_shape=jax.ShapeDtypeStruct((9, 528, 256), bf16),
        in_specs=[vm, vm, vm, pl.BlockSpec(memory_space=pl.ANY)],
        out_specs=pl.BlockSpec(memory_space=pl.ANY),
        scratch_shapes=[
            V((12, 4096, 128), bf16), V((1024, 128), f32), V((3072, 128), f32),
            V((12, 256, 128), bf16), V((12, 256, 128), bf16), V((3072, 128), f32),
            V((256, 384), bf16), V((4, 512, 128), f32), V((592, 512), bf16),
            V((16, 512), bf16), V((16, 512), bf16),
            V((16, 512), bf16), V((16, 128), bf16), V((16, 128), bf16),
            V((16, 512), bf16), V((16, 128), bf16), V((16, 128), bf16),
            V((9, 2, 544, 128), f32), V((9, 528, 256), bf16),
            D((12,)), D((12,)), D((12,)), D((8,)), D((8,)), D((9,)), D((2,)),
        ],
        compiler_params=pltpu.CompilerParams(
            collective_id=0, has_side_effects=True, vmem_limit_bytes=56 * 1024 * 1024
        ),
        name="gather",
    )(source, routes, window, weights)


UNROLL = 4

def conv_kernel(lhs, sw, sb, mw, mb, out, tmat, ma, ml, mr, lv, h32, r0, r1, r2, r3, h32b, y32, y32b, o0, o1, o2, o3, lsem, sems):
    f32, bf16 = jnp.float32, jnp.bfloat16
    band, n_band = lax.axis_index("band"), lax.axis_size("band")

    def load(w):
        return pltpu.make_async_copy(lhs.at[w], lv.at[w], lsem.at[w])

    for w in range(9):
        load(w).start()

    sw32 = sw[...].astype(f32)
    for j in range(4):
        for y in range(2):
            top = 2 * j + y
            pieces = []
            for b in range(3):
                if top > 0:
                    pieces.append(jnp.zeros((8 * top, 128), f32))
                for a in range(3):
                    pieces.append(sw32[(3 * a + b) * 8 : (3 * a + b) * 8 + 8])
                if top < 7:
                    pieces.append(jnp.zeros((8 * (7 - top), 128), f32))
            pieces.append(jnp.zeros((16, 128), f32))
            tmat[j, :, y * 128 : y * 128 + 128] = jnp.concatenate(pieces, axis=0).astype(bf16)
    for a in range(3):
        row = a * 256
        ma[row : row + 128, 0:128] = mw[3 * a + 1]
        ma[row : row + 128, 128:256] = mw[3 * a]
        ma[row + 128 : row + 256, 0:128] = mw[3 * a + 2]
        ma[row + 128 : row + 256, 128:256] = mw[3 * a + 1]
    for side, b in ((ml, 0), (mr, 2)):
        for r in range(4):
            for o in range(2):
                a = r - o
                block = mw[3 * a + b] if 0 <= a <= 2 else jnp.zeros((128, 128), bf16)
                side[r * 128 : r * 128 + 128, o * 128 : o * 128 + 128] = block

    hb = sb[...] * 0.5
    bias = mb[...]

    def stem(pair, ring, h32):
        w = pair // 4
        acc = jnp.dot(lv[w, 0:520], tmat[pair - w * 4], preferred_element_type=f32)
        for y in range(2):
            u = acc[:, y * 128 : y * 128 + 128] * 0.5 + hb
            h = u + u * jnp.tanh(u)
            row = 2 * pair + y
            gone = jnp.logical_or(
                jnp.logical_and(band == 0, row == 0), jnp.logical_and(band == n_band - 1, row == 65)
            )
            h32[y] = h * jnp.where(gone, 0.0, 1.0)
            for i, start in enumerate((1, 2, 0, 3)):
                ring[y, :, i * 128 : i * 128 + 128] = h32[y, pl.ds(start, 256, stride=2), :].astype(bf16)

    def mix(lo, hi, ob, y32):
        rows = (lo.at[0], lo.at[1], hi.at[0], hi.at[1])
        left = jnp.dot(
            jnp.concatenate([r[:, 256:384] for r in rows], axis=1), ml[...], preferred_element_type=f32
        )
        right = jnp.dot(
            jnp.concatenate([r[:, 384:512] for r in rows], axis=1), mr[...], preferred_element_type=f32
        )
        for o in range(2):
            both = jnp.dot(
                jnp.concatenate([r[:, 0:256] for r in rows[o : o + 3]], axis=1), ma[...], preferred_element_type=f32
            )
            cut = slice(o * 128, o * 128 + 128)
            y32[o, pl.ds(0, 256, stride=2), :] = both[:, 0:128] + left[:, cut] + bias
            y32[o, pl.ds(1, 256, stride=2), :] = both[:, 128:256] + right[:, cut] + bias
            ob[o] = y32[o].astype(bf16)

    rings = (r0, r1, r2, r3)
    obs = (o0, o1, o2, o3)
    hs = (h32, h32b)
    ys = (y32, y32b)
    load(0).wait()
    for pair in range(3):
        stem(jnp.int32(pair), rings[pair], hs[pair % 2])
    for w in range(1, 9):
        load(w).wait()

    def put(p, i):
        return pltpu.make_async_copy(obs[i], out.at[pl.ds(2 * p, 2)], sems.at[i])

    def body(t, carry):
        for i in range(UNROLL):
            p = UNROLL * t + i
            if i < 4:
                @pl.when(t > 0)
                def _():
                    put(p - 4, i % 4).wait()
            else:
                put(p - 4, i % 4).wait()
            stem(p + 3, rings[(i + 3) % 4], hs[(i + 1) % 2])
            mix(rings[i % 4], rings[(i + 1) % 4], obs[i % 4], ys[i % 2])
            put(p, i % 4).start()
        return carry

    lax.fori_loop(0, 32 // UNROLL, body, 0)
    for i in range(4):
        put(28 + i, i).wait()


def conv(lhs, sw, sb, mw, mb):
    V = pltpu.VMEM
    bf16, f32 = jnp.bfloat16, jnp.float32
    vm = pl.BlockSpec(memory_space=pltpu.VMEM)
    return pl.pallas_call(
        conv_kernel,
        out_shape=jax.ShapeDtypeStruct((64, 512, 128), bf16),
        in_specs=[pl.BlockSpec(memory_space=pl.ANY)] + [vm] * 4,
        out_specs=pl.BlockSpec(memory_space=pl.ANY),
        scratch_shapes=[
            V((4, 256, 256), bf16), V((768, 256), bf16), V((512, 256), bf16), V((512, 256), bf16),
            V((9, 528, 256), bf16), V((2, 520, 128), f32),
            V((2, 256, 512), bf16), V((2, 256, 512), bf16), V((2, 256, 512), bf16), V((2, 256, 512), bf16),
            V((2, 520, 128), f32), V((2, 512, 128), f32), V((2, 512, 128), f32),
            V((2, 512, 128), bf16), V((2, 512, 128), bf16), V((2, 512, 128), bf16), V((2, 512, 128), bf16),
            pltpu.SemaphoreType.DMA((9,)), pltpu.SemaphoreType.DMA((4,)),
        ],
        compiler_params=pltpu.CompilerParams(vmem_limit_bytes=56 * 1024 * 1024),
        name="conv",
    )(lhs, sw, sb, mw, mb)


def on_device(source, routes, slot_weights, window, stem_weight, stem_bias, mix_weight, mix_bias):
    columns = gather(source, routes.T, window.transpose(1, 0, 2), slot_weights.reshape(12, 4096, 128))
    return conv(
        columns,
        stem_weight.reshape(72, 128),
        stem_bias.reshape(1, 128),
        mix_weight,
        mix_bias.reshape(1, 128),
    )


def solution(mesh):
    in_specs = (
        P(("band", "lon"), None, None),
        P(("band", "lon"), None),
        P(("band", "lon"), None, None, None, None),
        P(("band", "lon"), None, None),
        P(),
        P(),
        P(),
        P(),
    )
    out_specs = P("band", "lon", None)
    return jax.shard_map(
        on_device, mesh=mesh, in_specs=in_specs, out_specs=out_specs, check_vma=False
    )
```

time: 57.3 us -> 48.6 us (0.85)
  Pallas kernels: 53.7 us -> 48.4 us
  local copies, waits for them, and re-layouts: 2.06 us -> 0 us
  other arithmetic: 1.33 us -> 0 us
    pallas_call x1, Pallas kernels: 32.3 us -> 27.9 us  [conv(): pl.pallas_call(conv_kernel, out_shape=jax.ShapeDtypeStruct((64, 512, 128)...]
    unnamed x1 -> x0, local copies, waits for them, and re-layouts: 1.41 us -> none
    pallas_call x1, Pallas kernels: 21.4 us -> 20.5 us  [gather(): pl.pallas_call(gather_kernel, out_shape=jax.ShapeDtypeStruct((9, 528, 256...]
    unnamed x1 -> x0, other arithmetic: 0.71 us -> none
    reshape x1 -> x0, local copies, waits for them, and re-layouts: 0.65 us -> none  [on_device(): window.reshape(1, 384)]
    convert_element_type x1 -> x0, other arithmetic: 0.62 us -> none  [on_device(): jnp.stack([band == 0, band == lax.axis_size('band') - 1]).astype(jnp.int32)]
where the time goes in v3:
time: 48.6 us; the launch traced here: 48.4 us
  Pallas kernels  48.4 us (100%)
    pallas_call x1, Pallas kernels, conv(): pl.pallas_call(conv_kernel, out_shape=jax.ShapeDtypeStruct((64, 512, 128)...  27.9 us
    pallas_call x1, Pallas kernels, gather(): pl.pallas_call(gather_kernel, out_shape=jax.ShapeDtypeStruct((9, 528, 256...  20.5 us

profile of v3, /device:TPU:96, one launch (start us, length us, event | category | flops | bytes accessed | tf_op | source)
XLA Modules:
  0.0 48.4 jit_solution(5804222757193200090)
XLA Ops:
  0.0 20.5 %gather.1.lhs = bf16[9,528,256]{2,1,0:T(8,128)(2,1)} custom-call(bf16[128,8,128]{2,1,0:T(8,128)(2,1)} %src.1, s32[2,128]{1,0:T(2,128)} %bitcast.9, s32[12,1,32]{2,1,0:T(1,128)} %bitcast.8, bf16[12,4096,128]{2,1,0:T(8,128)(2,1)} %bitcast.6), custom_call_target="tpu_custom_call" | custom-call | tf_op jit(solution)/shard_map/gather/pallas_call | solution.py:286
  20.6 27.9 %conv.1 = bf16[64,512,128]{2,1,0:T(8,128)(2,1)} custom-call(bf16[9,528,256]{2,1,0:T(8,128)(2,1)} %gather.1.lhs, bf16[72,128]{1,0:T(8,128)(2,1)} %bitcast.7, f32[1,128]{1,0:T(1,128)} %bitcast.10, bf16[9,128,128]{2,1,0:T(8,128)(2,1)} %mw.1, f32[1,128]{1,0:T(1,128)} %bitcast.11), custom_call_target="tpu_custom_call" | custom-call | tf_op jit(solution)/shard_map/conv/pallas_call | solution.py:417

commit v4 on v3

--- a/solution.py
+++ b/solution.py
@@ -8,8 +8,8 @@
 NT = (((1,), (1,)), ((), ()))
 
 
-def gather_kernel(src, routes, window, weights, out, wv, s32, o32, sendb, recvb, c32, place, fs32, fe, colr, coll,
-                  lc, ln, ls, rc, rn, rs, y32, lv, w_sem, send_sem, recv_sem, hs_sem, hr_sem, o_sem, e_sem):
+def gather_kernel(src_hbm, routes_hbm, window_hbm, weights, out, src, routes, window, wv, s32, o32, sendb, recvb, c32, place, fs32, fe, colr, coll,
+                  lc, ln, ls, rc, rn, rs, y32, lv, w_sem, send_sem, recv_sem, hs_sem, hr_sem, o_sem, e_sem, i_sem):
     f32, bf16 = jnp.float32, jnp.bfloat16
     n_band, n_lon = lax.axis_size("band"), lax.axis_size("lon")
     band, lon = lax.axis_index("band"), lax.axis_index("lon")
@@ -37,6 +37,12 @@
         ok = inside(target)
         return jnp.logical_and(ok, jnp.logical_or(edge(band), edge(target))) if q % 4 == 2 else ok
 
+    inputs = [
+        pltpu.make_async_copy(source, target, i_sem.at[i])
+        for i, (source, target) in enumerate(((src_hbm, src), (routes_hbm, routes), (window_hbm, window)))
+    ]
+    for c in inputs:
+        c.start()
     others = [q for q in range(12) if q != 4]
     count = jnp.int32(0)
     for q in others:
@@ -45,7 +51,7 @@
             pl.semaphore_signal(barrier, inc=1, device_id=there(q), device_id_type=pl.DeviceIdType.MESH)
         count = count + greets(q).astype(jnp.int32)
 
-    order = (4, 0, 8, 5, 7, 1, 3, 9, 11, 6, 2, 10)
+    order = (4, 0, 8, 1, 3, 9, 11, 5, 7, 2, 10, 6)
 
     def fetch(q):
         return pltpu.make_async_copy(weights.at[q], wv.at[q], w_sem.at[q])
@@ -53,6 +59,7 @@
     for q in order:
         fetch(q).start()
 
+    inputs[1].wait()
     code = lax.broadcasted_iota(jnp.int32, (16, 128), 0)
     names = jnp.logical_or(routes[0:1, :] == code, routes[1:2, :] == code)
     earlier = lax.broadcasted_iota(jnp.int32, (128, 128), 0) < lax.broadcasted_iota(jnp.int32, (128, 128), 1)
@@ -64,6 +71,7 @@
     select = jnp.concatenate(
         [(jnp.broadcast_to(ranked[q : q + 1], (32, 128)) == slot).astype(f32) for q in range(12)], axis=0
     ).astype(bf16)
+    inputs[0].wait()
     s32[...] = src[...].astype(f32).reshape(1024, 128)
     for f in range(0, 8, 2):
         planes = jnp.concatenate(
@@ -83,13 +91,14 @@
             device_id=there(q), device_id_type=pl.DeviceIdType.MESH,
         )
 
-    for q in (2, 6, 10, 1, 3, 9, 11, 5, 7, 0, 8):
+    for q in (2, 6, 10, 1, 3, 0, 8, 9, 11, 5, 7):
         @pl.when(sends(q))
         def _():
             route(q).start()
 
     spot = lax.broadcasted_iota(jnp.int32, (256, 384), 0)
     wanted = lax.rem(spot, 64) * 4 + lax.div(spot, 64)
+    inputs[2].wait()
     lands = jnp.concatenate([window[q] for q in range(12)], axis=1)
     place[...] = (jnp.broadcast_to(lands, (256, 384)) == wanted).astype(f32).astype(bf16)
     zero_rows = jnp.zeros((16, 512), bf16)
@@ -219,22 +228,32 @@
         shift(w, 16, 480)
         body_out(w).start()
 
+    def arrive(copies):
+        for c in copies:
+            c.wait_recv()
+
     @pl.when(band < n_band - 1)
     def _():
-        for c in up:
-            c.wait_recv()
+        arrive(up[2:])
 
     @pl.when(band > 0)
     def _():
-        for c in down:
-            c.wait_recv()
-
-    for c in side:
-        c.wait_recv()
+        arrive(down[2:])
+
     for w in (0, 8):
         turn(w)
         shift(w, 16, 480)
         body_out(w).start()
+
+    arrive(side)
+
+    @pl.when(band < n_band - 1)
+    def _():
+        arrive(up[:2])
+
+    @pl.when(band > 0)
+    def _():
+        arrive(down[:2])
 
     lane = lax.broadcasted_iota(jnp.int32, (16, 640), 1)
     blank = jnp.zeros((16, 512), f32)
@@ -282,13 +301,13 @@
 def gather(source, routes, window, weights):
     V, D = pltpu.VMEM, pltpu.SemaphoreType.DMA
     bf16, f32 = jnp.bfloat16, jnp.float32
-    vm = pl.BlockSpec(memory_space=pltpu.VMEM)
     return pl.pallas_call(
         gather_kernel,
         out_shape=jax.ShapeDtypeStruct((9, 528, 256), bf16),
-        in_specs=[vm, vm, vm, pl.BlockSpec(memory_space=pl.ANY)],
+        in_specs=[pl.BlockSpec(memory_space=pl.ANY)] * 4,
         out_specs=pl.BlockSpec(memory_space=pl.ANY),
         scratch_shapes=[
+            V((128, 8, 128), bf16), V((2, 128), jnp.int32), V((12, 1, 32), jnp.int32),
             V((12, 4096, 128), bf16), V((1024, 128), f32), V((3072, 128), f32),
             V((12, 256, 128), bf16), V((12, 256, 128), bf16), V((3072, 128), f32),
             V((256, 384), bf16), V((4, 512, 128), f32), V((592, 512), bf16),
@@ -296,7 +315,7 @@
             V((16, 512), bf16), V((16, 128), bf16), V((16, 128), bf16),
             V((16, 512), bf16), V((16, 128), bf16), V((16, 128), bf16),
             V((9, 2, 544, 128), f32), V((9, 528, 256), bf16),
-            D((12,)), D((12,)), D((12,)), D((8,)), D((8,)), D((9,)), D((2,)),
+            D((12,)), D((12,)), D((12,)), D((8,)), D((8,)), D((9,)), D((2,)), D((3,)),
         ],
         compiler_params=pltpu.CompilerParams(
             collective_id=0, has_side_effects=True, vmem_limit_bytes=56 * 1024 * 1024
@@ -306,6 +325,8 @@
 
 
 UNROLL = 4
+MC = 128
+SC = 256
 
 def conv_kernel(lhs, sw, sb, mw, mb, out, tmat, ma, ml, mr, lv, h32, r0, r1, r2, r3, h32b, y32, y32b, o0, o1, o2, o3, lsem, sems):
     f32, bf16 = jnp.float32, jnp.bfloat16
@@ -347,9 +368,9 @@
     hb = sb[...] * 0.5
     bias = mb[...]
 
-    def stem(pair, ring, h32):
+    def stem(pair, h32, m, size):
         w = pair // 4
-        acc = jnp.dot(lv[w, 0:520], tmat[pair - w * 4], preferred_element_type=f32)
+        acc = jnp.dot(lv[w, m : m + size], tmat[pair - w * 4], preferred_element_type=f32)
         for y in range(2):
             u = acc[:, y * 128 : y * 128 + 128] * 0.5 + hb
             h = u + u * jnp.tanh(u)
@@ -357,12 +378,17 @@
             gone = jnp.logical_or(
                 jnp.logical_and(band == 0, row == 0), jnp.logical_and(band == n_band - 1, row == 65)
             )
-            h32[y] = h * jnp.where(gone, 0.0, 1.0)
+            h32[y, m : m + size] = h * jnp.where(gone, 0.0, 1.0)
+
+    def split(ring, h32, m, size):
+        for y in range(2):
             for i, start in enumerate((1, 2, 0, 3)):
-                ring[y, :, i * 128 : i * 128 + 128] = h32[y, pl.ds(start, 256, stride=2), :].astype(bf16)
-
-    def mix(lo, hi, ob, y32):
-        rows = (lo.at[0], lo.at[1], hi.at[0], hi.at[1])
+                ring[y, m : m + size, i * 128 : i * 128 + 128] = h32[
+                    y, pl.ds(2 * m + start, size, stride=2), :
+                ].astype(bf16)
+
+    def mix(lo, hi, ob, y32, m, size):
+        rows = [r[k, m : m + size, :] for r in (lo, hi) for k in range(2)]
         left = jnp.dot(
             jnp.concatenate([r[:, 256:384] for r in rows], axis=1), ml[...], preferred_element_type=f32
         )
@@ -374,9 +400,23 @@
                 jnp.concatenate([r[:, 0:256] for r in rows[o : o + 3]], axis=1), ma[...], preferred_element_type=f32
             )
             cut = slice(o * 128, o * 128 + 128)
-            y32[o, pl.ds(0, 256, stride=2), :] = both[:, 0:128] + left[:, cut] + bias
-            y32[o, pl.ds(1, 256, stride=2), :] = both[:, 128:256] + right[:, cut] + bias
-            ob[o] = y32[o].astype(bf16)
+            y32[o, pl.ds(2 * m, size, stride=2), :] = both[:, 0:128] + left[:, cut] + bias
+            y32[o, pl.ds(2 * m + 1, size, stride=2), :] = both[:, 128:256] + right[:, cut] + bias
+            ob[o, 2 * m : 2 * m + 2 * size] = y32[o, 2 * m : 2 * m + 2 * size].astype(bf16)
+
+    def both(stem_args, mix_args):
+        cuts = [(k * SC, SC if k < 512 // SC - 1 else SC + 8) for k in range(512 // SC)]
+        done = 0
+        for k in range(256 // MC):
+            if mix_args:
+                mix(*mix_args, k * MC, MC)
+            if stem_args:
+                n = len(cuts) * MC // 256
+                for m, size in cuts[k * n : k * n + n]:
+                    stem(stem_args[0], stem_args[1], m, size)
+        if stem_args:
+            for k in range(256 // MC):
+                split(stem_args[2], stem_args[1], k * MC, MC)
 
     rings = (r0, r1, r2, r3)
     obs = (o0, o1, o2, o3)
@@ -384,7 +424,7 @@
     ys = (y32, y32b)
     load(0).wait()
     for pair in range(3):
-        stem(jnp.int32(pair), rings[pair], hs[pair % 2])
+        both((jnp.int32(pair), hs[pair % 2], rings[pair]), None)
     for w in range(1, 9):
         load(w).wait()
 
@@ -400,8 +440,7 @@
                     put(p - 4, i % 4).wait()
             else:
                 put(p - 4, i % 4).wait()
-            stem(p + 3, rings[(i + 3) % 4], hs[(i + 1) % 2])
-            mix(rings[i % 4], rings[(i + 1) % 4], obs[i % 4], ys[i % 2])
+            both((p + 3, hs[(i + 1) % 2], rings[(i + 3) % 4]), (rings[i % 4], rings[(i + 1) % 4], obs[i % 4], ys[i % 2]))
             put(p, i % 4).start()
         return carry
 

time: 48.6 us -> 45.7 us (0.940)
  Pallas kernels: 48.4 us -> 45.2 us
    pallas_call x1, Pallas kernels: 20.5 us -> 18.9 us  [gather(): pl.pallas_call(gather_kernel, out_shape=jax.ShapeDtypeStruct((9, 528, 256...]
    pallas_call x1, Pallas kernels: 27.9 us -> 26.3 us  [conv(): pl.pallas_call(conv_kernel, out_shape=jax.ShapeDtypeStruct((64, 512, 128)...]
where the time goes in v4:
time: 45.7 us; the launch traced here: 45.2 us
  Pallas kernels  45.2 us (99%)
    pallas_call x1, Pallas kernels, conv(): pl.pallas_call(conv_kernel, out_shape=jax.ShapeDtypeStruct((64, 512, 128)...  26.3 us
    pallas_call x1, Pallas kernels, gather(): pl.pallas_call(gather_kernel, out_shape=jax.ShapeDtypeStruct((9, 528, 256...  18.9 us

profile of v4, /device:TPU:96, one launch (start us, length us, event | category | flops | bytes accessed | tf_op | source)
XLA Modules:
  0.0 45.2 jit_solution(3164805138893256262)
XLA Ops:
  0.0 18.9 %gather.1.lhs = bf16[9,528,256]{2,1,0:T(8,128)(2,1)} custom-call(bf16[128,8,128]{2,1,0:T(8,128)(2,1)} %src_hbm.1, s32[2,128]{1,0:T(2,128)} %bitcast.9, s32[12,1,32]{2,1,0:T(1,128)} %bitcast.8, bf16[12,4096,128]{2,1,0:T(8,128)(2,1)} %bitcast.6), custom_call_target="tpu_custom_call" | custom-call | tf_op jit(solution)/shard_map/gather/pallas_call | solution.py:304
  18.9 26.3 %conv.1 = bf16[64,512,128]{2,1,0:T(8,128)(2,1)} custom-call(bf16[9,528,256]{2,1,0:T(8,128)(2,1)} %gather.1.lhs, bf16[72,128]{1,0:T(8,128)(2,1)} %bitcast.7, f32[1,128]{1,0:T(1,128)} %bitcast.10, bf16[9,128,128]{2,1,0:T(8,128)(2,1)} %mw.1, f32[1,128]{1,0:T(1,128)} %bitcast.11), custom_call_target="tpu_custom_call" | custom-call | tf_op jit(solution)/shard_map/conv/pallas_call | solution.py:456
